TPU v7x, 32 devices: a whole 2x2x4 slice. The times are simulated.
32 devices in a mesh: dp: 16 (over z, x, core), head: 2 (over y).
Axes of the slice: x: 2, y: 2, z: 4, core: 2. Of those that a mesh axis runs over, the one named last changes fastest.
Arguments:
- patches: bfloat16 [32, 1024, 768], P('dp'), may hold values from -6 to 6
- keep_mask: int32 [32, 1024], P('dp'), may hold values 0 or 1
- counts: int32 [32], P('dp'), may hold values from 196 to 1024, as said below
- ln_gain: float32 [768], replicated, may hold values from 0.1 to 1.9
- w_in: bfloat16 [2, 768, 2688], P('head'), may hold values from -0.21875 to 0.21875
- q_gain: float32 [12, 64], P('head'), may hold values from 0.1 to 1.9
- k_gain: float32 [12, 64], P('head'), may hold values from 0.1 to 1.9
- w_out: bfloat16 [2, 1920, 768], P('head')
- d_out: bfloat16 [32, 1024, 768], P('dp'), may hold values from -6 to 6
Outputs:
- block_output: bfloat16 [32, 1024, 768], P('dp')
- d_in: bfloat16 [32, 1024, 768], P('dp')
- g_ln: float32 [768], P('dp')
- g_w_in: float32 [2, 768, 2688], P('head', 'dp')
- g_q: float32 [12, 64], P('head', 'dp')
- g_k: float32 [12, 64], P('head', 'dp')
- g_w_out: float32 [2, 1920, 768], P('head', None, 'dp')
Inputs may be any that keep to these rules, and one draw needn't show every extreme that they name: `counts`: each count is 196, 576 or 1024; the first image's is 1024.
All inputs are finite; a program needn't handle non-finite values. No bound on the sum of `keep_mask` on one device may be relied on, other than what follows from the above.
Results may differ from a plain program's by a relative error of at most 0.0091.
Values sent between devices are 32-bit elements; how exact they have to be, the bound alone decides.
A program may use at most 256 MiB of HBM per device.

v0:
```python
import functools
import math

import jax
import jax.numpy as jnp
from jax import lax
from jax.experimental import pallas as pl
from jax.experimental.pallas import tpu as pltpu
from jax.sharding import PartitionSpec as P

EPS = 1e-06
LOG2E = 1.4426950408889634
F32 = jnp.float32
BF16 = jnp.bfloat16
VMEM = 67000000
COST = 560
BQ = 512
UNROLL = 1
NT = (((1,), (1,)), ((), ()))
NN = (((1,), (0,)), ((), ()))


def cost(us):
    return pl.CostEstimate(flops=int(us * COST * 1e6), bytes_accessed=1, transcendentals=0)


def mm(a, b, dims=NN):
    return lax.dot_general(a, b, dims, preferred_element_type=F32)


def gelu_parts(u):
    cdf = 0.5 + 0.5 * lax.erf(u * math.sqrt(0.5))
    return u * cdf, cdf + u * (jnp.exp2(u * u * (-0.5 * LOG2E)) * (1.0 / math.sqrt(2.0 * math.pi)))


def head_norm(v, gain, heads, hdim):
    tokens = v.shape[-1]
    v = v.reshape(heads, hdim, tokens)
    centre = v - jnp.mean(v, axis=1, keepdims=True)
    r = lax.rsqrt(jnp.mean(centre * centre, axis=1, keepdims=True) + EPS)
    n = (centre * r).reshape(heads * hdim, tokens)
    return (n * gain).astype(BF16), r


def layer_norm(x_ref, lng_ref):
    x = x_ref[...].astype(F32)
    centre = x - jnp.mean(x, axis=-1, keepdims=True)
    r = lax.rsqrt(jnp.mean(centre * centre, axis=-1, keepdims=True) + EPS)
    return (centre * r * lng_ref[...]).astype(BF16)


def project_kernel(heads, hdim, first_ref, x_ref, dz_ref, lng_ref, win_ref, wout_ref, qg_ref, kg_ref,
                   left_ref, qt_ref, kt_ref, vt_ref, dot_ref, rq_ref, rk_ref, right_ref, wt_ref, xn_ref):
    inner = heads * hdim
    now = lax.rem(pl.program_id(0), 2)

    @pl.when(pl.program_id(0) == 0)
    def _():
        wt_ref[...] = win_ref[:, : 3 * inner].T
        xn_ref[0] = layer_norm(first_ref, lng_ref)

    xn = xn_ref[now]
    xn_ref[1 - now] = layer_norm(x_ref, lng_ref)
    dz = dz_ref[...]
    width = dz.shape[1]
    left_ref[:width, :] = dz.T
    left_ref[width:, :] = xn.T
    qkv = mm(wt_ref[...], xn, NT)
    qn, rq = head_norm(qkv[:inner], qg_ref[...], heads, hdim)
    kn, rk = head_norm(qkv[inner : 2 * inner], kg_ref[...], heads, hdim)
    qt_ref[...] = qn
    kt_ref[...] = kn
    rq_ref[...] = rq
    rk_ref[...] = rk
    vt_ref[...] = qkv[2 * inner :].astype(BF16)
    dot_ref[...] = mm(wout_ref[:inner, :], dz, NT).astype(BF16)
    hidden = win_ref.shape[1] - 3 * inner
    step = 512
    for c in range(0, hidden, step):
        u = mm(xn, win_ref[:, 3 * inner + c : 3 * inner + c + step])
        dh = mm(dz, wout_ref[inner + c : inner + c + step, :], NT)
        h, slope = gelu_parts(u)
        right_ref[:, c : c + step] = h.astype(BF16)
        right_ref[:, hidden + c : hidden + c + step] = (dh * slope).astype(BF16)


def project(x, dz, lng, win, wout, qg, kg, heads, hdim, tm=256):
    tokens, width = x.shape
    inner = heads * hdim
    gw = win.shape[1]
    hidden = gw - 3 * inner
    steps = tokens // tm
    given = lambda f: pl.BlockSpec((tm, width), lambda i: (f(i), 0))
    col = lambda n: pl.BlockSpec((n, tm), lambda i: (0, i))
    whole = lambda a: pl.BlockSpec(a.shape, lambda i: (0,) * a.ndim, pipeline_mode=pl.Buffered(1))
    stat = pl.BlockSpec((heads, 1, tm), lambda i: (0, 0, i))
    sds = jax.ShapeDtypeStruct
    return pl.pallas_call(
        functools.partial(project_kernel, heads, hdim),
        grid=(steps,),
        in_specs=[given(lambda i: 0), given(lambda i: jnp.minimum(i + 1, steps - 1)), given(lambda i: i), whole(lng), whole(win), whole(wout), whole(qg), whole(kg)],
        out_specs=[col(2 * width), col(inner), col(inner), col(inner), col(inner), stat, stat, pl.BlockSpec((tm, 2 * hidden), lambda i: (i, 0))],
        out_shape=[sds((2 * width, tokens), BF16)]
        + [sds((inner, tokens), BF16)] * 4
        + [sds((heads, 1, tokens), F32)] * 2
        + [sds((tokens, 2 * hidden), BF16)],
        scratch_shapes=[pltpu.VMEM((3 * inner, width), BF16), pltpu.VMEM((2, tm, width), BF16)],
        compiler_params=pltpu.CompilerParams(vmem_limit_bytes=VMEM),
        cost_estimate=cost(28),
        name="project",
    )(x, x, dz, lng, win, wout, qg, kg)


def attend_kernel(hdim, bq, nh, image_ref, qt_ref, kt_ref, vt_ref, dot_ref, rq_ref, rk_ref, vrow_ref, qg_ref, kg_ref,
                  o_ref, dq_ref, dk_ref, dv_ref, gq_ref, gk_ref, dqt_s, dkt_s, dvt_s, ot_s, kn_s, ktv_s, vs_s, va_s):
    tokens = qt_ref.shape[1]
    vrow = vrow_ref[0]
    vrow_b = vrow.astype(BF16)
    scale = hdim ** (-0.5)
    sub = lax.broadcasted_iota(jnp.int32, (16, tokens), 0)
    ones_row = jnp.where(sub == 0, jnp.broadcast_to(vrow, (16, tokens)), 0.0).astype(BF16)
    minus_row = jnp.where(sub < 2, 1.0, 0.0).astype(BF16)
    ktv_s[...] = kt_ref[...] * vrow_b
    for h in range(nh):
        rows = slice(h * hdim, (h + 1) * hdim)
        vt = vt_ref[rows, :]
        kn_s[h] = kt_ref[rows, :].T
        vs_s[h, :hdim, :] = vt * vrow_b
        vs_s[h, hdim:, :] = ones_row
        va_s[h] = jnp.concatenate([vt, minus_row], axis=0).T
    dkt_s[...] = jnp.zeros_like(dkt_s)
    dvt_s[...] = jnp.zeros_like(dvt_s)
    sub16 = lax.broadcasted_iota(jnp.int32, (16, bq), 0)

    def first(h, i):
        rows = slice(h * hdim, (h + 1) * hdim)
        at = pl.ds(pl.multiple_of(i * bq, bq), bq)
        return jnp.exp2(mm(kn_s[h], qt_ref[rows, at])).astype(BF16)

    def second(h, i, e):
        rows = slice(h * hdim, (h + 1) * hdim)
        at = pl.ds(pl.multiple_of(i * bq, bq), bq)
        qb = qt_ref[rows, at]
        dob = dot_ref[rows, at]
        oa = mm(vs_s[h], e)
        linv = 1.0 / oa[hdim : hdim + 1, :]
        o = oa[:hdim, :] * linv
        ot_s[rows, at] = o.astype(BF16)
        dof = dob.astype(F32)
        delta = jnp.sum(dof * o, axis=0, keepdims=True) * linv
        hi = delta.astype(BF16)
        lo = (delta - hi.astype(F32)).astype(BF16)
        dos = (dof * linv).astype(BF16)
        minus = jnp.where(sub16 == 0, -hi.astype(F32), jnp.where(sub16 == 1, -lo.astype(F32), 0.0)).astype(BF16)
        t = mm(va_s[h], jnp.concatenate([dos, minus], axis=0))
        ds = (e.astype(F32) * t).astype(BF16)
        dvt_s[rows, :] += mm(dos, e, NT)
        dkt_s[rows, :] += mm(qb, ds, NT)
        dqt_s[rows, at] = mm(ktv_s[rows, :], ds)

    def block(i, _):
        es = [first(h, i) for h in range(nh)]
        for h in range(nh):
            second(h, i, es[h])
        return 0

    lax.fori_loop(0, tokens // bq, block, 0, unroll=UNROLL)

    for p in range(nh // 2):
        prow = slice(p * 2 * hdim, (p + 1) * 2 * hdim)
        o_ref[:, prow] = ot_s[prow, :].T
        dv_ref[:, prow] = (dvt_s[prow, :] * vrow).astype(BF16).T
        for src, raw, r_ref, g_ref, grad_ref, dst, mul, c in (
            (dqt_s, qt_ref, rq_ref, qg_ref, gq_ref, dq_ref, scale, scale * LOG2E),
            (dkt_s, kt_ref, rk_ref, kg_ref, gk_ref, dk_ref, 1.0 / LOG2E, 1.0),
        ):
            both = []
            for h in (2 * p, 2 * p + 1):
                rows = slice(h * hdim, (h + 1) * hdim)
                g = g_ref[rows, :]
                inv = 1.0 / (g * c)
                d = src[rows, :]
                if raw is kt_ref:
                    d = d * vrow
                x = raw[rows, :].astype(F32)
                prod = d * x
                grad_ref[rows, :] = jnp.sum(prod, axis=1, keepdims=True) * (inv * mul)
                a = d * (g * mul)
                m1 = jnp.mean(a, axis=0, keepdims=True)
                m2 = jnp.mean(prod, axis=0, keepdims=True) * (mul / c)
                both.append((r_ref[h] * (a - m1 - (x * inv) * m2)).astype(BF16))
            dst[:, prow] = jnp.concatenate(both, axis=0).T

def attend(image, qt, kt, vt, dot, rq, rk, vrow, qg, kg, heads, hdim, slots, bq=BQ, nh=2):
    inner = heads * hdim
    w = nh * hdim
    sds = jax.ShapeDtypeStruct
    tcol = pl.BlockSpec((w, slots), lambda p, im: (p, im[0]))
    stat = pl.BlockSpec((nh, 1, slots), lambda p, im: (p, 0, im[0]))
    gain = pl.BlockSpec((w, 1), lambda p, im: (p, 0))
    row = pl.BlockSpec((slots, w), lambda p, im: (0, p))
    return pl.pallas_call(
        functools.partial(attend_kernel, hdim, min(bq, slots), nh),
        grid_spec=pltpu.PrefetchScalarGridSpec(
            num_scalar_prefetch=1,
            grid=(heads // nh,),
            in_specs=[tcol, tcol, tcol, tcol, stat, stat, pl.BlockSpec((1, 1, slots), lambda p, im: (im[0], 0, 0)), gain, gain],
            out_specs=[row, row, row, row, gain, gain],
            scratch_shapes=[pltpu.VMEM((w, slots), F32)] * 3
            + [
                pltpu.VMEM((w, slots), BF16),
                pltpu.VMEM((nh, slots, hdim), BF16),
                pltpu.VMEM((w, slots), BF16),
                pltpu.VMEM((nh, hdim + 16, slots), BF16),
                pltpu.VMEM((nh, slots, hdim + 16), BF16),
            ],
        ),
        out_shape=[sds((slots, inner), BF16)] * 4 + [sds((inner, 1), F32)] * 2,
        compiler_params=pltpu.CompilerParams(vmem_limit_bytes=VMEM),
        cost_estimate=cost(25),
        name="attend",
    )(image, qt, kt, vt, dot, rq, rk, vrow, qg, kg)


def overlaps(cuts, step, tm):
    for k in range(len(cuts) - 1):
        low, high = max(step * tm, cuts[k]), min((step + 1) * tm, cuts[k + 1])
        if low < high:
            yield k, low - cuts[k], low - step * tm, high - low


def back_rows_kernel(inner, cuts, steps, image_ref, dq_ref, dk_ref, dv_ref, du_ref, w_ref, *outs):
    g = (
        mm(dq_ref[...], w_ref[:, :inner], NT)
        + mm(dk_ref[...], w_ref[:, inner : 2 * inner], NT)
        + mm(dv_ref[...], w_ref[:, 2 * inner : 3 * inner], NT)
        + mm(du_ref[...], w_ref[:, 3 * inner :], NT)
    )
    if len(outs) == 1:
        outs[0][...] = g
        return
    for step in range(steps):

        @pl.when(pl.program_id(0) == step)
        def _(step=step):
            for k, at, low, n in overlaps(cuts, step, g.shape[0]):
                outs[k][at : at + n, :] = g[low : low + n]


def back_rows(image, dq, dk, dv, right, win, cuts, tm=256):
    slots, inner = dq.shape
    width, gw = win.shape
    hidden = gw - 3 * inner
    steps = slots // tm
    row = lambda n: pl.BlockSpec((tm, n), lambda i, im: (i, 0))
    parts = [b - a for a, b in zip(cuts, cuts[1:])]
    return pl.pallas_call(
        functools.partial(back_rows_kernel, inner, cuts, steps),
        grid_spec=pltpu.PrefetchScalarGridSpec(
            num_scalar_prefetch=1,
            grid=(steps,),
            in_specs=[row(inner)] * 3 + [pl.BlockSpec((tm, hidden), lambda i, im: (im[0] * steps + i, 1)), pl.BlockSpec(win.shape, lambda i, im: (0, 0), pipeline_mode=pl.Buffered(1))],
            out_specs=[pl.BlockSpec((n, width), lambda i, im: (0, 0)) for n in parts] if len(parts) > 1 else [row(width)],
        ),
        out_shape=[jax.ShapeDtypeStruct((n, width), F32) for n in parts],
        compiler_params=pltpu.CompilerParams(vmem_limit_bytes=VMEM),
        cost_estimate=cost(10),
        name="back_rows",
    )(image, dq, dk, dv, right, win)


def fetch(me, parts, stage, sem):
    rows = stage.shape[0] // len(parts)
    for k, refs in enumerate(parts):
        block = jnp.bitwise_xor(me, k)
        low = 0
        for ref in refs:
            pltpu.make_async_copy(ref, stage.at[pl.ds(pl.multiple_of(block * rows + low, 8), ref.shape[0])], sem.at[block]).start()
            low += ref.shape[0]


def grouped(counts, refs):
    out = []
    for n in counts:
        out.append(refs[:n])
        refs = refs[n:]
    return out


def arrived(block, rows, stage, sem):
    view = stage.at[pl.ds(pl.multiple_of(block * rows, 8), rows)]
    pltpu.make_async_copy(view, view, sem.at[block]).wait()


def unpack_kernel(counts, me_ref, *refs):
    parts, (out_ref, stage, sem) = grouped(counts, refs[:-3]), refs[-3:]
    step = pl.program_id(0)
    rows = out_ref.shape[0]

    @pl.when(step == 0)
    def _():
        fetch(me_ref[0], parts, stage, sem)

    arrived(step, rows, stage, sem)
    out_ref[...] = stage[pl.ds(pl.multiple_of(step * rows, 8), rows), :].astype(BF16)


def unpack(me, parts):
    pieces = len(parts)
    flat = [v for part in parts for v in part]
    rows, n = sum(v.shape[0] for v in parts[0]), flat[0].shape[1]
    return pl.pallas_call(
        functools.partial(unpack_kernel, tuple(len(part) for part in parts)),
        grid_spec=pltpu.PrefetchScalarGridSpec(
            num_scalar_prefetch=1,
            grid=(pieces,),
            in_specs=[pl.BlockSpec(memory_space=pl.ANY)] * len(flat),
            out_specs=pl.BlockSpec((rows, n), lambda i, me: (i, 0)),
            scratch_shapes=[pltpu.VMEM((rows * pieces, n), F32), pltpu.SemaphoreType.DMA((pieces,))],
        ),
        out_shape=jax.ShapeDtypeStruct((rows * pieces, n), BF16),
        compiler_params=pltpu.CompilerParams(vmem_limit_bytes=VMEM),
        cost_estimate=cost(6),
        name="unpack",
    )(me, *flat)


def heads_fwd_kernel(heads, hdim, me_ref, qg_ref, kg_ref, xnt_ref, *refs):
    parts, (qt_ref, kt_ref, vt_ref, wo_ref, _, _, wt_ref, stage, sem) = refs[:-9], refs[-9:]
    inner = heads * hdim

    @pl.when(pl.program_id(0) == 0)
    def _():
        fetch(me_ref[0], [(ref,) for ref in parts], stage, sem)
        for k in range(len(parts)):
            arrived(k, parts[0].shape[0], stage, sem)
        wt_ref[...] = stage[:, : 3 * inner].astype(BF16).T
        wo_ref[...] = stage[:, 3 * inner :].astype(BF16)

    qkv = mm(wt_ref[...], xnt_ref[...])
    qt_ref[...] = head_norm(qkv[:inner], qg_ref[...], heads, hdim)[0]
    kt_ref[...] = head_norm(qkv[inner : 2 * inner], kg_ref[...], heads, hdim)[0]
    vt_ref[...] = qkv[2 * inner :].astype(BF16)


def heads_fwd(me, qg, kg, left, parts, heads, hdim, tm=512):
    width, tokens = left.shape[0] // 2, left.shape[1]
    inner = heads * hdim
    n = parts[0].shape[1]
    col = pl.BlockSpec((inner, tm), lambda i, me: (0, i))
    gain = pl.BlockSpec((inner, 1), lambda i, me: (0, 0))
    out = pl.BlockSpec((width, inner), lambda i, me: (0, 0))
    raw = pl.BlockSpec(memory_space=pl.ANY)
    sds = jax.ShapeDtypeStruct
    return pl.pallas_call(
        functools.partial(heads_fwd_kernel, heads, hdim),
        grid_spec=pltpu.PrefetchScalarGridSpec(
            num_scalar_prefetch=1,
            grid=(tokens // tm,),
            in_specs=[gain, gain, pl.BlockSpec((width, tm), lambda i, me: (1, i))] + [raw] * len(parts),
            out_specs=[col, col, col, out, raw, raw],
            scratch_shapes=[pltpu.VMEM((3 * inner, width), BF16), pltpu.VMEM((width, n), F32), pltpu.SemaphoreType.DMA((len(parts),))],
        ),
        out_shape=[sds((inner, tokens), BF16)] * 3 + [sds((width, inner), BF16)] + [sds((tokens, width), BF16)] * 2,
        compiler_params=pltpu.CompilerParams(vmem_limit_bytes=VMEM),
        cost_estimate=cost(10),
        name="heads_fwd",
    )(me, qg, kg, left, *parts)


def attend_fwd_kernel(hdim, bq, nh, qt_ref, kt_ref, vt_ref, vrow_ref, o_ref, ot_s, kn_s, vs_s):
    tokens = qt_ref.shape[1]
    vrow = vrow_ref[0]
    vrow_b = vrow.astype(BF16)
    sub = lax.broadcasted_iota(jnp.int32, (16, tokens), 0)
    ones_row = jnp.where(sub == 0, jnp.broadcast_to(vrow, (16, tokens)), 0.0).astype(BF16)
    for h in range(nh):
        rows = slice(h * hdim, (h + 1) * hdim)
        kn_s[h] = kt_ref[rows, :].T
        vs_s[h, :hdim, :] = vt_ref[rows, :] * vrow_b
        vs_s[h, hdim:, :] = ones_row

    def block(i, _):
        at = pl.ds(pl.multiple_of(i * bq, bq), bq)
        es = [jnp.exp2(mm(kn_s[h], qt_ref[h * hdim : (h + 1) * hdim, at])).astype(BF16) for h in range(nh)]
        for h in range(nh):
            oa = mm(vs_s[h], es[h])
            ot_s[h * hdim : (h + 1) * hdim, at] = (oa[:hdim, :] * (1.0 / oa[hdim : hdim + 1, :])).astype(BF16)
        return 0

    lax.fori_loop(0, tokens // bq, block, 0, unroll=True)
    o_ref[...] = ot_s[...].T


def attend_fwd(qt, kt, vt, vrow, heads, hdim, slots, bq=BQ, nh=2):
    inner = heads * hdim
    w = nh * hdim
    seqs = qt.shape[1] // slots
    tcol = pl.BlockSpec((w, slots), lambda s, p: (p, s))
    return pl.pallas_call(
        functools.partial(attend_fwd_kernel, hdim, min(bq, slots), nh),
        grid=(seqs, heads // nh),
        in_specs=[tcol, tcol, tcol, pl.BlockSpec((1, 1, slots), lambda s, p: (s, 0, 0))],
        out_specs=pl.BlockSpec((slots, w), lambda s, p: (s, p)),
        out_shape=jax.ShapeDtypeStruct((seqs * slots, inner), BF16),
        scratch_shapes=[pltpu.VMEM((w, slots), BF16), pltpu.VMEM((nh, slots, hdim), BF16), pltpu.VMEM((nh, hdim + 16, slots), BF16)],
        compiler_params=pltpu.CompilerParams(vmem_limit_bytes=VMEM),
        cost_estimate=cost(16),
        name="attend_fwd",
    )(qt, kt, vt, vrow)


def out_rows_kernel(inner, cuts, steps, image_ref, x_ref, dz_ref, lng_ref, w_ref, wa_ref, wb_ref, o_ref, hid_ref, of_ref, *refs):
    pieces = len(cuts) - 1
    near, far = refs[:pieces], refs[pieces : 2 * pieces]
    out_ref, din_ref, both, sem = refs[-4:]
    tm = x_ref.shape[0]
    now = pl.program_id(0)

    @pl.when(now == 0)
    def _():
        for step in range(steps):
            for k, at, low, n in overlaps(cuts, step, tm):
                for side, parts in enumerate((near, far)):
                    pltpu.make_async_copy(parts[k].at[pl.ds(at, n)], both.at[step, side, pl.ds(low, n)], sem.at[step]).start()

    x = x_ref[...].astype(F32)
    centre = x - jnp.mean(x, axis=-1, keepdims=True)
    r = lax.rsqrt(jnp.mean(centre * centre, axis=-1, keepdims=True) + EPS)
    n = centre * r
    scaled = n * lng_ref[...]
    xn = scaled.astype(BF16)
    hidden = wb_ref.shape[1] // 2
    total = mm(o_ref[...], w_ref[:inner, :]) + mm(hid_ref[...], w_ref[inner:, :]) + mm(of_ref[...], wa_ref[...], NT)
    parts = []
    for c in range(0, hidden, 512):
        parts.append(gelu_parts(mm(xn, wb_ref[:, c : c + 512]))[0].astype(BF16))
    total = total + mm(jnp.concatenate(parts, axis=1), wb_ref[:, hidden:], NT)
    out_ref[...] = (x + total).astype(BF16)
    pltpu.make_async_copy(both.at[now], both.at[now], sem.at[now]).wait()
    a = (both[now, 0] + both[now, 1]) * lng_ref[...]
    back = r * (a - jnp.mean(a, axis=-1, keepdims=True) - n * jnp.mean(a * n, axis=-1, keepdims=True))
    din_ref[...] = (dz_ref[...].astype(F32) + back).astype(BF16)


def out_rows(image, x, dz, lng, wout, wa, wb, o, right, of, near, far, cuts, prior, tm=256):
    slots, inner = o.shape
    go, width = wout.shape
    steps = slots // tm
    row = lambda n: pl.BlockSpec((tm, n), lambda i, im: (i, 0))
    of_image = lambda n: pl.BlockSpec((tm, n), lambda i, im: (im[0] * steps + i, 0))
    at = of_image(width)
    whole = lambda a: pl.BlockSpec(a.shape, lambda i, im: (0,) * a.ndim, pipeline_mode=pl.Buffered(1))
    given = [image, x, dz, lng, wout, wa, wb, o, right, of, *near, *far]
    raw = pl.BlockSpec(memory_space=pl.ANY)
    return pl.pallas_call(
        functools.partial(out_rows_kernel, inner, cuts, steps),
        grid_spec=pltpu.PrefetchScalarGridSpec(
            num_scalar_prefetch=1,
            grid=(steps,),
            in_specs=[at, at, whole(lng), whole(wout), whole(wa), whole(wb), row(inner), of_image(go - inner), of_image(inner)] + [raw] * (len(near) + len(far) + 2),
            out_specs=[at, at],
            scratch_shapes=[pltpu.VMEM((steps, 2, tm, width), F32), pltpu.SemaphoreType.DMA((steps,))],
        ),
        out_shape=[jax.ShapeDtypeStruct(x.shape, BF16)] * 2,
        input_output_aliases={len(given) + k: k for k in range(2)},
        compiler_params=pltpu.CompilerParams(vmem_limit_bytes=VMEM),
        cost_estimate=cost(18),
        name="out_rows",
    )(*given, *prior)


def early_kernel(left_ref, right_ref, out_ref):
    out_ref[...] = mm(left_ref[...], right_ref[...])


def early_grads(left, right, tn=512):
    width, tokens = left.shape[0] // 2, left.shape[1]
    both = right.shape[1]
    steps = both // tn
    return pl.pallas_call(
        early_kernel,
        grid=(steps,),
        in_specs=[pl.BlockSpec((width, tokens), lambda j: (jnp.where(j < steps // 2, 0, 1), 0)), pl.BlockSpec((tokens, tn), lambda j: (0, j))],
        out_specs=pl.BlockSpec((width, tn), lambda j: (0, j)),
        out_shape=jax.ShapeDtypeStruct((width, both), F32),
        compiler_params=pltpu.CompilerParams(vmem_limit_bytes=VMEM),
        cost_estimate=cost(16),
        name="early_grads",
    )(left, right)


def late_kernel(seqs, low, core_ref, *refs):
    dzt, xnt = refs[:seqs], refs[seqs : 2 * seqs]
    o, dq, dk, dv = (refs[(2 + k) * seqs : (3 + k) * seqs] for k in range(4))
    small, keep, send = refs[-3:]
    width = o[0].shape[1]

    def store(cols, v):
        for half in range(2):
            rows = jnp.concatenate([v[b : b + low] for b in range(half * low, v.shape[0], 2 * low)], axis=0)

            @pl.when(core_ref[0] == half)
            def _():
                keep[:, cols] = rows

            @pl.when(core_ref[0] != half)
            def _():
                send[:, cols] = rows

    for k, (left, right) in enumerate(((dzt, o), (xnt, dq), (xnt, dk), (xnt, dv))):
        store(slice(k * width, (k + 1) * width), sum(mm(left[s][...], right[s][...]) for s in range(seqs)))
    store(slice(4 * width, 4 * width + small.shape[1]), small[...])


def late_grads(core, left, o, dq, dk, dv, small, low):
    seqs = len(o)
    slots, inner = o[0].shape
    width = left.shape[0] // 2
    tm = 4 * low
    while tm < 192:
        tm *= 2
    steps = width // tm
    above = [pl.BlockSpec((tm, slots), lambda i, c, s=s: (i, s)) for s in range(seqs)]
    below = [pl.BlockSpec((tm, slots), lambda i, c, s=s: (steps + i, s)) for s in range(seqs)]
    whole = pl.BlockSpec((slots, inner), lambda i, c: (0, 0), pipeline_mode=pl.Buffered(1))
    wide = 4 * inner + small.shape[1]
    out = pl.BlockSpec((tm // 2, wide), lambda i, c: (i, 0))
    return pl.pallas_call(
        functools.partial(late_kernel, seqs, low),
        grid_spec=pltpu.PrefetchScalarGridSpec(
            num_scalar_prefetch=1,
            grid=(steps,),
            in_specs=above + below + [whole] * (4 * seqs) + [pl.BlockSpec((tm, small.shape[1]), lambda i, c: (i, 0))],
            out_specs=[out, out],
        ),
        out_shape=[jax.ShapeDtypeStruct((width // 2, wide), F32)] * 2,
        compiler_params=pltpu.CompilerParams(vmem_limit_bytes=VMEM),
        cost_estimate=cost(12),
        name="late_grads",
    )(core, *[left] * (2 * seqs), *o, *dq, *dk, *dv, small)


def gate(value, *done):
    return lax.optimization_barrier((value, *done))[0]


def small_terms(g_q, g_k, width, shards):
    heads, hdim = g_q.shape
    part = lambda v: v.reshape(heads, shards, hdim // shards).transpose(1, 0, 2).reshape(shards, -1)
    gains = jnp.concatenate([part(g_q), part(g_k)], axis=1)
    gains = jnp.pad(gains, ((0, 0), (0, width // shards - gains.shape[1]))).reshape(width, 1)
    return jnp.pad(gains, ((0, 0), (0, 127)))


def per_device(shards, patches, keep_mask, counts, ln_gain, w_in, q_gain, k_gain, w_out, d_out):
    seqs, slots, width = patches.shape
    heads, hdim = q_gain.shape
    inner = heads * hdim
    swap = [(0, 1), (1, 0)]
    scale = hdim ** (-0.5)
    win, wout = w_in[0], w_out[0]
    hidden = wout.shape[0] - inner
    x = patches.reshape(seqs * slots, width)
    dz = d_out.reshape(seqs * slots, width)
    slot_ids = jnp.arange(slots, dtype=jnp.int32)
    valid = (slot_ids[None, :] < counts[:, None]) & ((keep_mask == 1) | (slot_ids[None, :] == 0))
    vrow = valid.astype(F32).reshape(seqs, 1, slots)
    qg = q_gain.reshape(inner, 1)
    kg = k_gain.reshape(inner, 1)
    lng = ln_gain.reshape(1, width)
    qgs = qg * (scale * LOG2E)
    across = lambda v: lax.ppermute(v, "head", swap)

    def pair(v, bit):
        return lax.ppermute(v, "dp", [(i, i ^ bit) for i in range(shards)])

    number = [jnp.full((1,), s, jnp.int32) for s in range(seqs)]
    me = lax.axis_index("dp")

    quarter = width // 4

    def rows_of(bit, left_cols, right_rows):
        mine = ((me // bit) % 2) + 2 * (me % 2)
        rows = lax.dynamic_slice(win, (mine * quarter, left_cols[0]), (quarter, left_cols[1] - left_cols[0]))
        cols = lax.dynamic_slice(wout, (right_rows[0], mine * quarter), (right_rows[1] - right_rows[0], quarter))
        return mine.astype(jnp.int32).reshape(1), jnp.concatenate([rows.astype(F32), cols.astype(F32).T], axis=1)

    mine_a, piece_a = rows_of(2, (0, 3 * inner), (0, inner))
    mine_b, piece_b = rows_of(4, (3 * inner, win.shape[1]), (inner, wout.shape[0]))
    gains = across(jnp.concatenate([qgs, kg], axis=0).reshape(-1, 128))
    a = [across(piece_a)]

    low = width // shards
    cell = lambda v, axis, at: lax.dynamic_index_in_dim(v, at, axis, False)
    others = shards // 4

    def by_two(v, w):
        bit = (me // 2) % 2
        v, w = (u.reshape(others, 2, low, -1) for u in (v, w))
        return cell(v, 1, bit) + cell(w, 1, bit), cell(v, 1, 1 - bit) + cell(w, 1, 1 - bit)

    def to_all(v):
        return [pair(cell(v, 0, (me // 4) ^ m), 4 * m) for m in range(1, others)]

    def heads_of(s, first):
        return attend(number[s], first, kt, vt, dot, rq, rk, vrow, qg, kg, heads, hdim, slots)

    left, qt, kt, vt, dot, rq, rk, right = project(x, dz, lng, win, wout, qgs, kg, heads, hdim)
    half = quarter // 2
    o0, dq0, dk0, dv0, gq0, gk0 = heads_of(0, gate(qt, *a, gains))
    b = [[across(gate(piece_b[:half], a[0]))]]
    a.append(pair(a[0], 2))
    cuts = (0, slots)
    n0 = back_rows(number[0], gate(dq0, a[1], *b[0]), dk0, dv0, right, win, cuts)
    b[0].append(across(gate(piece_b[half:], dq0)))
    a += [pair(gate(v, dq0), 1) for v in a]
    b.append([pair(b[0][0], 4)])
    f0 = [across(gate(n0[0], b[0][1]))]
    early = early_grads(gate(left, *n0), right)
    early = gate(early, b[0][1], b[1][0])
    early_rs = lax.psum_scatter(early, "dp", scatter_dimension=0, tiled=True)
    b[1].append(pair(b[0][1], 4))
    o1, dq1, dk1, dv1, gq1, gk1 = heads_of(1, gate(qt, early))
    n1 = back_rows(number[1], gate(dq1, b[1][1], *a), dk1, dv1, right, win, (0, slots))
    b += [[pair(gate(v, dq1), 1) for v in part] for part in b]
    small = small_terms((gq0 + gq1).reshape(heads, hdim), (gk0 + gk1).reshape(heads, hdim), width, shards)
    core = (me % 2).astype(jnp.int32).reshape(1)
    keep, send = late_grads(core, gate(left, *n1), [o0, o1], [dq0, dq1], [dk0, dk1], [dv0, dv1], small, low)
    send = gate(send, *b[2], *b[3], f0[0])
    f1 = [across(gate(v, send)) for v in n1]
    got = pair(send, 1)
    wb = unpack(mine_b, [(gate(b[0][0], send), b[0][1])] + b[1:])
    keep, send = by_two(keep, gate(got, wb))
    got = pair(send, 2)
    gains = gains.reshape(-1, 1)
    qf, kf, vf, wa, *blank = heads_fwd(mine_a, gate(gains[:inner], send), gains[inner:], left, a, heads, hdim)
    of = attend_fwd(qf, kf, vf, vrow, heads, hdim, slots)
    keep = keep + gate(got, of)
    got = to_all(keep)
    outs = out_rows(number[0], gate(x, keep), dz, lng, wout, wa, wb, o0, right, of, n0, f0, cuts, blank)
    late_rs = cell(keep, 0, me // 4) + sum(gate(v, outs[0]) for v in got)
    bo, d_in = out_rows(number[1], gate(x, outs[0], *f1), dz, lng, wout, wa, wb, o1, right, of, n1, f1, (0, slots), outs)
    block_output = bo.reshape(patches.shape)
    d_in = d_in.reshape(patches.shape)
    g_w_out = jnp.concatenate([late_rs[:, :inner], early_rs[:, :hidden]], axis=1).T[None]
    g_w_in = jnp.concatenate([late_rs[:, inner : 4 * inner], early_rs[:, hidden:]], axis=1)[None]
    band = lambda v: lax.dynamic_slice_in_dim(v, me * (width // shards), width // shards, 0)
    g_ln = jnp.sum(band(win).astype(F32) * g_w_in[0], axis=1) / band(ln_gain)
    g_ln = g_ln + across(g_ln)
    terms = late_rs[:, 4 * inner]
    count = inner // shards
    g_q = terms[:count].reshape(heads, hdim // shards)
    g_k = terms[count : 2 * count].reshape(heads, hdim // shards)
    return block_output, d_in, g_ln, g_w_in, g_q, g_k, g_w_out


def solution(mesh):
    placed = (
        P("dp", None, None),
        P("dp", None),
        P("dp"),
        P(),
        P("head", None, None),
        P("head", None),
        P("head", None),
        P("head", None, None),
        P("dp", None, None),
    )
    return jax.shard_map(
        functools.partial(per_device, mesh.shape["dp"]),
        mesh=mesh,
        in_specs=placed,
        out_specs=(
            P("dp", None, None),
            P("dp", None, None),
            P("dp"),
            P("head", "dp", None),
            P("head", "dp"),
            P("head", "dp"),
            P("head", None, "dp"),
        ),
        check_vma=False,
    )
```

profile of v0, /device:TPU:0, one launch (start us, length us, event | category | flops | bytes accessed | tf_op | source)
XLA Modules:
  0.0 289.1 jit_solution(8971141538080562082)
XLA Ops:
  7.2 0.8 reshape.120
  8.0 0.8 reshape.138.qg_ref
  9.0 3.0 %collective-permute-start.1 = (f32[6,128]{1,0:T(8,128)S(1)}, f32[6,128]{1,0:T(8,128)S(1)}, u32[]{:S(2)}, u32[]{:S(2)}) collective-permute-start(f32[6,128]{1,0:T(8,128)S(1)} %bitcast.93), channel_id=1, source_target_pairs={{0,1},{1,0},{2,3},{3,2},{4,5},{5,4},{6,7},{7,6},{8,9},{9,8},{10,11... | collective-permute-start | bytes 9224 | tf_op jit(solution)/shard_map/ppermute | solution.py:573
  12.1 1.1 constant_dynamic-slice_fusion.1
  13.3 1.1 dynamic-slice_bitcast_fusion.1
  14.3 1.2 maximum_convert_fusion.1
  15.6 0.8 copy.69.kg_ref
  16.4 1.9 dynamic-slice_bitcast_fusion
  18.3 1.6 constant_dynamic-slice_fusion
  20.5 1.1 copy.74
  21.6 24.0 %project.1 = (bf16[1536,2048]{1,0:T(8,128)(2,1)}, bf16[384,2048]{1,0:T(8,128)(2,1)}, bf16[384,2048]{1,0:T(8,128)(2,1)}, bf16[384,2048]{1,0:T(8,128)(2,1)}, bf16[...) custom-call(bf16[2048,768]{1,0:T(8,128)(2,1)} %bitcast.75, ...), custom_call_target="tpu_custom_call" | custom-call | flops 15680000000 | bytes 1 | tf_op jit(solution)/shard_map/project/pallas_call | solution.py:98
  45.6 1.5 maximum_convert_fusion
  47.2 1.5 fusion.4
  49.4 2.0 collective-permute-start.3
  51.4 1.5 collective-permute-start.2
  52.9 26.6 %attend.2 = (bf16[1024,384]{1,0:T(8,128)(2,1)}, bf16[1024,384]{1,0:T(8,128)(2,1)}, bf16[1024,384]{1,0:T(8,128)(2,1)}, bf16[1024,384]{1,0:T(8,128)(2,1)}, f32[384,1]{1,0:T(8,128)}, /*index=5*/f32[384,1]{1,0:T(8,128)}) custom-call(s32[1]{0:T(128)} %constant.99.clone.1.image_ref, bf16[384,2048]{1,0:T(8,128)(2,1)} %get-tuple-element.83.qt_ref, ...), custom_call_target="tpu_custom_call" | custom-call | flops 14000000000 | bytes 1 | tf_op jit(solution)/shard_map/attend/pallas_call | solution.py:202
  80.1 1.6 collective-permute-start.5
  81.7 9.6 %back_rows.2.refs_0_ = f32[1024,768]{1,0:T(8,128)} custom-call(s32[1]{0:T(128)} %constant.99.clone.1.image_ref, bf16[1024,384]{1,0:T(8,128)(2,1)} %get-tuple-element.76.dq_ref.refs_6_, bf16[1024,384]{1,0:T(8,128)(2,1)} %get-tuple-element.77.dk_ref.refs_8_, bf16[1024,384]{1,0:T(8,128)(2,1)} %get-tuple-element.78.dv_ref.refs_10_, ...), custom_call_target="tpu_custom_call" | custom-call | flops 5600000000 | bytes 1 | tf_op jit(solution)/shard_map/back_rows/pallas_call | solution.py:257
  91.3 16.3 %early_grads.1 = f32[768,3072]{1,0:T(8,128)} custom-call(bf16[1536,2048]{1,0:T(8,128)(2,1)} %get-tuple-element.90.left_ref.refs_0_.refs_1_.refs_2_.refs_3_.xnt_ref, bf16[2048,3072]{1,0:T(8,128)(2,1)} %get-tuple-element.79.du_ref.right_ref.hid_ref), custom_call_target="tpu_custom_call" | custom-call | flops 8960000000 | bytes 1 | tf_op jit(solution)/shard_map/early_grads/pallas_call | solution.py:481
  107.6 1.6 collective-permute-start.13
  110.2 26.9 %attend.3 = (bf16[1024,384]{1,0:T(8,128)(2,1)}, bf16[1024,384]{1,0:T(8,128)(2,1)}, bf16[1024,384]{1,0:T(8,128)(2,1)}, bf16[1024,384]{1,0:T(8,128)(2,1)}, f32[384,1]{1,0:T(8,128)}, /*index=5*/f32[384,1]{1,0:T(8,128)}) custom-call(s32[1]{0:T(128)} %constant.98.clone.1.image_ref, bf16[384,2048]{1,0:T(8,128)(2,1)} %get-tuple-element.83.qt_ref, ...), custom_call_target="tpu_custom_call" | custom-call | flops 14000000000 | bytes 1 | tf_op jit(solution)/shard_map/attend/pallas_call | solution.py:202
  137.9 1.4 add_reduce_fusion
  141.0 0.9 reshape.139
  141.9 9.7 %back_rows.3.refs_0_ = f32[1024,768]{1,0:T(8,128)} custom-call(s32[1]{0:T(128)} %constant.98.clone.1.image_ref, bf16[1024,384]{1,0:T(8,128)(2,1)} %get-tuple-element.87.dq_ref.refs_7_, bf16[1024,384]{1,0:T(8,128)(2,1)} %get-tuple-element.88.dk_ref.refs_9_, bf16[1024,384]{1,0:T(8,128)(2,1)} %get-tuple-element.89.dv_ref.refs_11_, ...), custom_call_target="tpu_custom_call" | custom-call | flops 5600000000 | bytes 1 | tf_op jit(solution)/shard_map/back_rows/pallas_call | solution.py:257
  151.6 1.8 pad.4.refs_12_
  153.3 14.5 %late_grads.1 = (f32[384,1664]{1,0:T(8,128)}, f32[384,1664]{1,0:T(8,128)}) custom-call(s32[1]{0:T(128)} %bitcast.1.core_ref, bf16[1536,2048]{1,0:T(8,128)(2,1)} %get-tuple-element.90.left_ref.refs_0_.refs_1_.refs_2_.refs_3_.xnt_ref, bf16[1536,2048]{1,0:T(8,128)(2,1)} %get-tuple-element.90.left_ref.refs_0_.refs_1_.refs_2_.refs_3_.xnt_ref, ...), custom_call_target="tpu_custom_call" | custom-call | flops 6720000000 | bytes 1 | tf_op jit(solution)/shard_map/late_grads/pallas_call | solution.py:529
  167.9 8.1 %collective-permute-done.13.refs_1_ = f32[1024,768]{1,0:T(8,128)} collective-permute-done((f32[1024,768]{1,0:T(8,128)}, f32[1024,768]{1,0:T(8,128)}, u32[]{:S(2)}, u32[]{:S(2)}) %collective-permute-start.13) | collective-permute-done | bytes 3145760 | tf_op jit(solution)/shard_map/ppermute | solution.py:573
  176.0 0.8 copy.92
  176.8 1.5 collective-permute-start.16
  178.3 6.0 %unpack.1.wb_ref = bf16[768,3072]{1,0:T(8,128)(2,1)} custom-call(s32[1]{0:T(128)} %bitcast.16.me_ref, f32[96,3072]{1,0:T(8,128)} %collective-permute-done.3.refs_0_, f32[96,3072]{1,0:T(8,128)} %collective-permute-done.4.refs_1_, f32[96,3072]{1,0:T(8,128)} %collective-permute-done.5.refs_2_, f32[96,3072]{1,0:T(8,128)} %collective-permute-done.6.refs_3_, ...), custom_call_target="tpu_custom_call" | custom-call | flops 3360000000 | bytes 1 | tf_op jit(solution)/shard_map/unpack/pallas_call | solution.py:312
  184.4 2.9 %add_bitcast_fusion = f32[4,48,1664]{2,1,0:T(8,128)} fusion(f32[4,2,48,1664]{3,2,1,0:T(8,128)} %bitcast.17, s32[]{:T(128)S(6)} %select_n.75, f32[4,2,48,1664]{3,2,1,0:T(8,128)} %bitcast.84), kind=kLoop, calls=%fused_computation.3 | loop fusion | flops 319488 | bytes 3833860 | tf_op jit(solution)/shard_map/add | solution.py:601
  187.7 0.8 copy.84.qg_ref
  188.5 10.8 %heads_fwd.1 = (bf16[384,2048]{1,0:T(8,128)(2,1)}, bf16[384,2048]{1,0:T(8,128)(2,1)}, bf16[384,2048]{1,0:T(8,128)(2,1)}, bf16[768,384]{1,0:T(8,128)(2,1)}, bf16[...) custom-call(s32[1]{0:T(128)} %bitcast.20.me_ref, f32[384,1]{1,0:T(8,128)} %copy.84.qg_ref, f32[384,1]{1,0:T(8,128)} %bitcast.88, ...), custom_call_target="tpu_custom_call" | custom-call | flops 5600000000 | bytes 1 | tf_op jit(solution)/shard_map/heads_fwd/pallas_call | solution.py:355
  199.3 14.5 %attend_fwd.1.of_ref = bf16[2048,384]{1,0:T(8,128)(2,1)} custom-call(bf16[384,2048]{1,0:T(8,128)(2,1)} %get-tuple-element.108.qt_ref, bf16[384,2048]{1,0:T(8,128)(2,1)} %get-tuple-element.109.kt_ref, bf16[384,2048]{1,0:T(8,128)(2,1)} %get-tuple-element.110.vt_ref, f32[2,1,1024]{2,1,0:T(1,128)} %reshape.136.vrow_ref), custom_call_target="tpu_custom_call" | custom-call | flops 8960000000 | bytes 1 | tf_op jit(solution)/shard_map/attend_fwd/pallas_call | solution.py:400
  213.8 10.5 %collective-permute-done.15 = f32[4,48,1664]{2,1,0:T(8,128)} collective-permute-done((f32[4,48,1664]{2,1,0:T(8,128)}, f32[4,48,1664]{2,1,0:T(8,128)}, u32[]{:S(2)}, u32[]{:S(2)}) %collective-permute-start.15) | collective-permute-done | bytes 1277984 | tf_op jit(solution)/shard_map/ppermute | solution.py:576
  224.2 2.2 fusion.1
  226.5 1.1 copy-done
  227.6 1.0 dynamic-slice_bitcast_fusion.3
  228.6 2.6 collective-permute-start.18
  231.2 0.8 collective-permute-start.19
  232.3 17.2 %out_rows.2 = (bf16[2048,768]{1,0:T(8,128)(2,1)}, bf16[2048,768]{1,0:T(8,128)(2,1)}) custom-call(s32[1]{0:T(128)} %constant.99.clone.1.image_ref, bf16[2048,768]{1,0:T(8,128)(2,1)} %bitcast.77, bf16[2048,768]{1,0:T(8,128)(2,1)} %bitcast.80, f32[1,768]{1,0:T(1,128)} %reshape.118.lng_ref, ...), custom_call_target="tpu_custom_call", output_to_operand_aliasing={{0}: (12, {}), {1}: (13, {})} | custom-call | flops 10080000000 | bytes 1 | tf_op jit(solution)/shard_map/out_rows/pallas_call | solution.py:456
  249.5 4.0 %collective-permute-done.18 = f32[48,1664]{1,0:T(8,128)} collective-permute-done((f32[48,1664]{1,0:T(8,128)}, f32[48,1664]{1,0:T(8,128)}, u32[]{:S(2)}, u32[]{:S(2)}) %collective-permute-start.18) | collective-permute-done | bytes 319520 | tf_op jit(solution)/shard_map/ppermute | solution.py:576
  254.1 1.3 bitcast_add_fusion.1
  257.8 17.2 %out_rows.3 = (bf16[2048,768]{1,0:T(8,128)(2,1)}, bf16[2048,768]{1,0:T(8,128)(2,1)}) custom-call(s32[1]{0:T(128)} %constant.98.clone.1.image_ref, bf16[2048,768]{1,0:T(8,128)(2,1)} %bitcast.78, bf16[2048,768]{1,0:T(8,128)(2,1)} %bitcast.81, f32[1,768]{1,0:T(1,128)} %reshape.118.lng_ref, ...), custom_call_target="tpu_custom_call", output_to_operand_aliasing={{0}: (12, {}), {1}: (13, {})} | custom-call | flops 10080000000 | bytes 1 | tf_op jit(solution)/shard_map/out_rows/pallas_call | solution.py:456
  275.1 1.1 fusion.5
  276.2 2.0 fusion.3
  278.8 0.8 maximum_bitcast_fusion
  279.6 2.2 collective-permute-done.20
  (73 shorter events, 10.7 us)
Async XLA Ops:
  7.2 267.9 %reduce-scatter.2.cloned.1.call-start = ((), (), s32[]{:S(2)}) async-start(), calls=%async_computation.1 | async-start | bytes 10027008 | tf_op jit(solution)/shard_map/reduce_scatter | solution.py:622
  8.8 6.7 %copy-start.2 = (f32[384,1]{1,0:T(8,128)}, f32[384,1]{1,0:T(8,128)S(1)}, u32[]{:S(2)}) copy-start(f32[384,1]{1,0:T(8,128)S(1)} %reshape.138.qg_ref) | copy-start | bytes 4612
  8.9 6.6 %copy-start.3 = (f32[384,1]{1,0:T(8,128)}, f32[384,1]{1,0:T(8,128)S(1)}, u32[]{:S(2)}) copy-start(f32[384,1]{1,0:T(8,128)S(1)} %broadcast_multiply_fusion.qg_ref) | copy-start | bytes 4612
  9.0 42.4 %collective-permute-start.1 = (f32[6,128]{1,0:T(8,128)S(1)}, f32[6,128]{1,0:T(8,128)S(1)}, u32[]{:S(2)}, u32[]{:S(2)}) collective-permute-start(f32[6,128]{1,0:T(8,128)S(1)} %bitcast.93), channel_id=1, source_target_pairs={{0,1},{1,0},{2,3},{3,2},{4,5},{5,4},{6,7},{7,6},{8,9},{9,8},{10,11... | collective-permute-start | bytes 9224 | tf_op jit(solution)/shard_map/ppermute | solution.py:573
  15.5 4.4 %copy-start.5 = (f32[768]{0:T(1024)S(1)}, f32[768]{0:T(1024)}, u32[]{:S(2)}) copy-start(f32[768]{0:T(1024)} %param.12) | copy-start | bytes 9220
  15.5 33.9 %collective-permute-start = (f32[192,1536]{1,0:T(8,128)}, f32[192,1536]{1,0:T(8,128)}, u32[]{:S(2)}, u32[]{:S(2)}) collective-permute-start(f32[192,1536]{1,0:T(8,128)} %maximum_convert_fusion.1), channel_id=1, source_target_pairs={{0,1},{1,0},{2,3},{3,2},{4,5},{5,4},{6,7},{7,6},{8,9},{9,8},{10,11... | collective-permute-start | bytes 3538952 | tf_op jit(solution)/shard_map/ppermute | solution.py:573
  47.1 1.6 copy-start.4
  47.2 1.6 copy-start.6
  49.4 30.7 %collective-permute-start.3 = (f32[96,3072]{1,0:T(8,128)}, f32[96,3072]{1,0:T(8,128)}, u32[]{:S(2)}, u32[]{:S(2)}) collective-permute-start(f32[96,3072]{1,0:T(8,128)} %get-tuple-element.75), channel_id=1, source_target_pairs={{0,1},{1,0},{2,3},{3,2},{4,5},{5,4},{6,7},{7,6},{8,9},{9,8},{10,11... | collective-permute-start | bytes 3538952 | tf_op jit(solution)/shard_map/ppermute | solution.py:573
  51.4 28.7 %collective-permute-start.2 = (f32[192,1536]{1,0:T(8,128)}, f32[192,1536]{1,0:T(8,128)}, u32[]{:S(2)}, u32[]{:S(2)}) collective-permute-start(f32[192,1536]{1,0:T(8,128)} %collective-permute-done.refs_0_), channel_id=1, source_target_pairs={{0,4},{2,6},{4,0},{6,2},{8,12},{10,14},{12,8},{14,10},{16,20},{18,... | collective-permute-start | bytes 3538952 | tf_op jit(solution)/shard_map/ppermute | solution.py:576
  79.5 28.1 %collective-permute-start.4 = (f32[96,3072]{1,0:T(8,128)}, f32[96,3072]{1,0:T(8,128)}, u32[]{:S(2)}, u32[]{:S(2)}) collective-permute-start(f32[96,3072]{1,0:T(8,128)} %get-tuple-element.81), channel_id=1, source_target_pairs={{0,1},{1,0},{2,3},{3,2},{4,5},{5,4},{6,7},{7,6},{8,9},{9,8},{10,11... | collective-permute-start | bytes 3538952 | tf_op jit(solution)/shard_map/ppermute | solution.py:573
  80.1 27.5 %collective-permute-start.5 = (f32[96,3072]{1,0:T(8,128)}, f32[96,3072]{1,0:T(8,128)}, u32[]{:S(2)}, u32[]{:S(2)}) collective-permute-start(f32[96,3072]{1,0:T(8,128)} %collective-permute-done.3.refs_0_), channel_id=1, source_target_pairs={{0,8},{2,10},{4,12},{6,14},{8,0},{10,2},{12,4},{14,6},{16,24},{18,... | collective-permute-start | bytes 3538952 | tf_op jit(solution)/shard_map/ppermute | solution.py:576
  107.6 68.4 %collective-permute-start.13 = (f32[1024,768]{1,0:T(8,128)}, f32[1024,768]{1,0:T(8,128)}, u32[]{:S(2)}, u32[]{:S(2)}) collective-permute-start(f32[1024,768]{1,0:T(8,128)} %back_rows.2.refs_0_), channel_id=1, source_target_pairs={{0,1},{1,0},{2,3},{3,2},{4,5},{5,4},{6,7},{7,6},{8,9},{9,8},{10,11... | collective-permute-start | bytes 9437192 | tf_op jit(solution)/shard_map/ppermute | solution.py:573
  109.2 31.2 %collective-permute-start.7 = (f32[192,1536]{1,0:T(8,128)}, f32[192,1536]{1,0:T(8,128)}, u32[]{:S(2)}, u32[]{:S(2)}) collective-permute-start(f32[192,1536]{1,0:T(8,128)} %collective-permute-done.refs_0_), channel_id=1, source_target_pairs={{0,2},{2,0},{4,6},{6,4},{8,10},{10,8},{12,14},{14,12},{16,18},{18,... | collective-permute-start | bytes 3538952 | tf_op jit(solution)/shard_map/ppermute | solution.py:576
  109.2 31.3 %collective-permute-start.8 = (f32[192,1536]{1,0:T(8,128)}, f32[192,1536]{1,0:T(8,128)}, u32[]{:S(2)}, u32[]{:S(2)}) collective-permute-start(f32[192,1536]{1,0:T(8,128)} %collective-permute-done.2.refs_1_), channel_id=1, source_target_pairs={{0,2},{2,0},{4,6},{6,4},{8,10},{10,8},{12,14},{14,12},{16,18},{18,... | collective-permute-start | bytes 3538952 | tf_op jit(solution)/shard_map/ppermute | solution.py:576
  109.7 28.2 %collective-permute-start.6 = (f32[96,3072]{1,0:T(8,128)}, f32[96,3072]{1,0:T(8,128)}, u32[]{:S(2)}, u32[]{:S(2)}) collective-permute-start(f32[96,3072]{1,0:T(8,128)} %collective-permute-done.4.refs_1_), channel_id=1, source_target_pairs={{0,8},{2,10},{4,12},{6,14},{8,0},{10,2},{12,4},{14,6},{16,24},{18,... | collective-permute-start | bytes 3538952 | tf_op jit(solution)/shard_map/ppermute | solution.py:576
  139.9 27.9 %collective-permute-start.9 = (f32[96,3072]{1,0:T(8,128)}, f32[96,3072]{1,0:T(8,128)}, u32[]{:S(2)}, u32[]{:S(2)}) collective-permute-start(f32[96,3072]{1,0:T(8,128)} %collective-permute-done.3.refs_0_), channel_id=1, source_target_pairs={{0,2},{2,0},{4,6},{6,4},{8,10},{10,8},{12,14},{14,12},{16,18},{18,... | collective-permute-start | bytes 3538952 | tf_op jit(solution)/shard_map/ppermute | solution.py:576
  139.9 27.9 %collective-permute-start.10 = (f32[96,3072]{1,0:T(8,128)}, f32[96,3072]{1,0:T(8,128)}, u32[]{:S(2)}, u32[]{:S(2)}) collective-permute-start(f32[96,3072]{1,0:T(8,128)} %collective-permute-done.4.refs_1_), channel_id=1, source_target_pairs={{0,2},{2,0},{4,6},{6,4},{8,10},{10,8},{12,14},{14,12},{16,18},{18,... | collective-permute-start | bytes 3538952 | tf_op jit(solution)/shard_map/ppermute | solution.py:576
  140.4 27.5 %collective-permute-start.11 = (f32[96,3072]{1,0:T(8,128)}, f32[96,3072]{1,0:T(8,128)}, u32[]{:S(2)}, u32[]{:S(2)}) collective-permute-start(f32[96,3072]{1,0:T(8,128)} %collective-permute-done.5.refs_2_), channel_id=1, source_target_pairs={{0,2},{2,0},{4,6},{6,4},{8,10},{10,8},{12,14},{14,12},{16,18},{18,... | collective-permute-start | bytes 3538952 | tf_op jit(solution)/shard_map/ppermute | solution.py:576
  140.5 27.4 %collective-permute-start.12 = (f32[96,3072]{1,0:T(8,128)}, f32[96,3072]{1,0:T(8,128)}, u32[]{:S(2)}, u32[]{:S(2)}) collective-permute-start(f32[96,3072]{1,0:T(8,128)} %collective-permute-done.6.refs_3_), channel_id=1, source_target_pairs={{0,2},{2,0},{4,6},{6,4},{8,10},{10,8},{12,14},{14,12},{16,18},{18,... | collective-permute-start | bytes 3538952 | tf_op jit(solution)/shard_map/ppermute | solution.py:576
  176.0 8.4 %collective-permute-start.14 = (f32[384,1664]{1,0:T(8,128)}, f32[384,1664]{1,0:T(8,128)}, u32[]{:S(2)}, u32[]{:S(2)}) collective-permute-start(f32[384,1664]{1,0:T(8,128)} %get-tuple-element.104), channel_id=1, source_target_pairs={{0,2},{2,0},{4,6},{6,4},{8,10},{10,8},{12,14},{14,12},{16,18},{18,... | collective-permute-start | bytes 7667720 | tf_op jit(solution)/shard_map/ppermute | solution.py:576
  176.8 72.7 %collective-permute-start.16 = (f32[1024,768]{1,0:T(8,128)}, f32[1024,768]{1,0:T(8,128)}, u32[]{:S(2)}, u32[]{:S(2)}) collective-permute-start(f32[1024,768]{1,0:T(8,128)} %back_rows.3.refs_0_), channel_id=1, source_target_pairs={{0,1},{1,0},{2,3},{3,2},{4,5},{5,4},{6,7},{7,6},{8,9},{9,8},{10,11... | collective-permute-start | bytes 9437192 | tf_op jit(solution)/shard_map/ppermute | solution.py:573
  187.3 37.0 %collective-permute-start.15 = (f32[4,48,1664]{2,1,0:T(8,128)}, f32[4,48,1664]{2,1,0:T(8,128)}, u32[]{:S(2)}, u32[]{:S(2)}) collective-permute-start(f32[4,48,1664]{2,1,0:T(8,128)} %add_bitcast_fusion), channel_id=1, source_target_pairs={{0,4},{2,6},{4,0},{6,2},{8,12},{10,14},{12,8},{14,10},{16,20},{18,... | collective-permute-start | bytes 3833864 | tf_op jit(solution)/shard_map/ppermute | solution.py:576
  226.5 1.1 copy-start
  228.6 24.9 %collective-permute-start.18 = (f32[48,1664]{1,0:T(8,128)}, f32[48,1664]{1,0:T(8,128)}, u32[]{:S(2)}, u32[]{:S(2)}) collective-permute-start(f32[48,1664]{1,0:T(8,128)} %get-tuple-element.157), channel_id=1, source_target_pairs={{0,16},{2,18},{4,20},{6,22},{8,24},{10,26},{12,28},{14,30},{16,0},... | collective-permute-start | bytes 958472 | tf_op jit(solution)/shard_map/ppermute | solution.py:576
  231.2 22.3 %collective-permute-start.19 = (f32[48,1664]{1,0:T(8,128)}, f32[48,1664]{1,0:T(8,128)}, u32[]{:S(2)}, u32[]{:S(2)}) collective-permute-start(f32[48,1664]{1,0:T(8,128)} %get-tuple-element.158), channel_id=1, source_target_pairs={{0,24},{2,26},{4,28},{6,30},{8,16},{10,18},{12,20},{14,22},{16,8},... | collective-permute-start | bytes 958472 | tf_op jit(solution)/shard_map/ppermute | solution.py:576
  232.0 22.1 %collective-permute-start.17 = (f32[48,1664]{1,0:T(8,128)}, f32[48,1664]{1,0:T(8,128)}, u32[]{:S(2)}, u32[]{:S(2)}) collective-permute-start(f32[48,1664]{1,0:T(8,128)} %get-tuple-element.159), channel_id=1, source_target_pairs={{0,8},{2,10},{4,12},{6,14},{8,0},{10,2},{12,4},{14,6},{16,24},{18,... | collective-permute-start | bytes 958472 | tf_op jit(solution)/shard_map/ppermute | solution.py:576
  255.4 0.8 copy-start.1
  275.0 3.8 %slice-start = ((f32[48,1664]{1,0:T(8,128)}), f32[48,384]{1,0:T(8,128)S(1)}, s32[]{:S(2)}) async-start(f32[48,1664]{1,0:T(8,128)} %copy-done.1), calls=%async_computation.2 | async-start | bytes 147456 | tf_op jit(solution)/shard_map/slice | solution.py:646
  278.2 3.6 %collective-permute-start.20 = (f32[48]{0:T(128)S(1)}, f32[48]{0:T(128)S(1)}, u32[]{:S(2)}, u32[]{:S(2)}) collective-permute-start(f32[48]{0:T(128)S(1)} %dynamic-slice_divide_fusion), channel_id=1, source_target_pairs={{0,1},{1,0},{2,3},{3,2},{4,5},{5,4},{6,7},{7,6},{8,9},{9,8},{10,11... | collective-permute-start | bytes 584 | tf_op jit(solution)/shard_map/ppermute | solution.py:573
Sparse Core Ops, SparseCore 0:
  107.7 115.6 reduce-scatter.1
where the time goes:
time: 294 us; the launch traced here: 289 us
  Pallas kernels  193 us (66%)
  waiting for transfers between devices  26.2 us (9%)
  local copies, waits for them, and re-layouts  22.7 us (8%)
  starting transfers between devices  18.6 us (6%)
  between operations  14.3 us (5%)
  other arithmetic  14.1 us (5%)
    pallas_call x2, Pallas kernels, attend(): pl.pallas_call(functools.partial(attend_kernel, hdim, min(bq, slots), nh)...  53.5 us
    pallas_call x2, Pallas kernels, out_rows(): pl.pallas_call(functools.partial(out_rows_kernel, inner, cuts, steps), gr...  34.4 us
    pallas_call x1, Pallas kernels, project(): pl.pallas_call(functools.partial(project_kernel, heads, hdim), grid=(step...  24 us
    pallas_call x2, Pallas kernels, back_rows(): pl.pallas_call(functools.partial(back_rows_kernel, inner, cuts, steps), g...  19.3 us
    pallas_call x1, Pallas kernels, early_grads(): pl.pallas_call(early_kernel, grid=(steps,), in_specs=[pl.BlockSpec((width...  16.3 us
    ppermute x14, waiting for transfers between devices, pair(): return lax.ppermute(v, 'dp', [(i, i ^ bit) for i in range(shards)])  15.9 us
    pallas_call x1, Pallas kernels, late_grads(): pl.pallas_call(functools.partial(late_kernel, seqs, low), grid_spec=pltpu...  14.5 us
    pallas_call x1, Pallas kernels, attend_fwd(): pl.pallas_call(functools.partial(attend_fwd_kernel, hdim, min(bq, slots),...  14.5 us
  transfers between devices with their start and end apart: 22, of which 6 were waited for; matrix products, arithmetic and copies ran while one was open for 10% of the time, Pallas kernels for 67%

commit v1 on v0

--- a/solution.py
+++ b/solution.py
@@ -510,7 +510,7 @@
 
     for k, (left, right) in enumerate(((dzt, o), (xnt, dq), (xnt, dk), (xnt, dv))):
         store(slice(k * width, (k + 1) * width), sum(mm(left[s][...], right[s][...]) for s in range(seqs)))
-    store(slice(4 * width, 4 * width + small.shape[1]), small[...])
+    store(slice(4 * width, 4 * width + 128), jnp.broadcast_to(small[...], (small.shape[0], 128)))
 
 
 def late_grads(core, left, o, dq, dk, dv, small, low):
@@ -524,14 +524,14 @@
     above = [pl.BlockSpec((tm, slots), lambda i, c, s=s: (i, s)) for s in range(seqs)]
     below = [pl.BlockSpec((tm, slots), lambda i, c, s=s: (steps + i, s)) for s in range(seqs)]
     whole = pl.BlockSpec((slots, inner), lambda i, c: (0, 0), pipeline_mode=pl.Buffered(1))
-    wide = 4 * inner + small.shape[1]
+    wide = 4 * inner + 128
     out = pl.BlockSpec((tm // 2, wide), lambda i, c: (i, 0))
     return pl.pallas_call(
         functools.partial(late_kernel, seqs, low),
         grid_spec=pltpu.PrefetchScalarGridSpec(
             num_scalar_prefetch=1,
             grid=(steps,),
-            in_specs=above + below + [whole] * (4 * seqs) + [pl.BlockSpec((tm, small.shape[1]), lambda i, c: (i, 0))],
+            in_specs=above + below + [whole] * (4 * seqs) + [pl.BlockSpec((tm, 1), lambda i, c: (i, 0))],
             out_specs=[out, out],
         ),
         out_shape=[jax.ShapeDtypeStruct((width // 2, wide), F32)] * 2,
@@ -543,14 +543,6 @@
 
 def gate(value, *done):
     return lax.optimization_barrier((value, *done))[0]
-
-
-def small_terms(g_q, g_k, width, shards):
-    heads, hdim = g_q.shape
-    part = lambda v: v.reshape(heads, shards, hdim // shards).transpose(1, 0, 2).reshape(shards, -1)
-    gains = jnp.concatenate([part(g_q), part(g_k)], axis=1)
-    gains = jnp.pad(gains, ((0, 0), (0, width // shards - gains.shape[1]))).reshape(width, 1)
-    return jnp.pad(gains, ((0, 0), (0, 127)))
 
 
 def per_device(shards, patches, keep_mask, counts, ln_gain, w_in, q_gain, k_gain, w_out, d_out):
@@ -589,7 +581,8 @@
     mine_a, piece_a = rows_of(2, (0, 3 * inner), (0, inner))
     mine_b, piece_b = rows_of(4, (3 * inner, win.shape[1]), (inner, wout.shape[0]))
     gains = across(jnp.concatenate([qgs, kg], axis=0).reshape(-1, 128))
-    a = [across(piece_a)]
+    split = quarter * 7 // 12
+    b = [[across(piece_b[:split])]]
 
     low = width // shards
     cell = lambda v, axis, at: lax.dynamic_index_in_dim(v, at, axis, False)
@@ -607,46 +600,47 @@
         return attend(number[s], first, kt, vt, dot, rq, rk, vrow, qg, kg, heads, hdim, slots)
 
     left, qt, kt, vt, dot, rq, rk, right = project(x, dz, lng, win, wout, qgs, kg, heads, hdim)
-    half = quarter // 2
-    o0, dq0, dk0, dv0, gq0, gk0 = heads_of(0, gate(qt, *a, gains))
-    b = [[across(gate(piece_b[:half], a[0]))]]
+    o0, dq0, dk0, dv0, gq0, gk0 = heads_of(0, gate(qt, *b[0], gains))
+    a = [across(gate(piece_a, *b[0]))]
+    b.append([pair(b[0][0], 4)])
+    cuts = (0, slots // 8, slots)
+    n0 = back_rows(number[0], gate(dq0, *a), dk0, dv0, right, win, cuts)
+    b[0].append(across(gate(piece_b[split:], *a)))
     a.append(pair(a[0], 2))
-    cuts = (0, slots)
-    n0 = back_rows(number[0], gate(dq0, a[1], *b[0]), dk0, dv0, right, win, cuts)
-    b[0].append(across(gate(piece_b[half:], dq0)))
-    a += [pair(gate(v, dq0), 1) for v in a]
-    b.append([pair(b[0][0], 4)])
-    f0 = [across(gate(n0[0], b[0][1]))]
+    f0 = [across(v) for v in n0]
     early = early_grads(gate(left, *n0), right)
-    early = gate(early, b[0][1], b[1][0])
+    early = gate(early, b[0][1], b[1][0], a[1], f0[0])
     early_rs = lax.psum_scatter(early, "dp", scatter_dimension=0, tiled=True)
     b[1].append(pair(b[0][1], 4))
     o1, dq1, dk1, dv1, gq1, gk1 = heads_of(1, gate(qt, early))
-    n1 = back_rows(number[1], gate(dq1, b[1][1], *a), dk1, dv1, right, win, (0, slots))
+    n1 = back_rows(number[1], gate(dq1, b[1][1]), dk1, dv1, right, win, (0, slots))
+    a += [pair(gate(v, dq1), 1) for v in a]
     b += [[pair(gate(v, dq1), 1) for v in part] for part in b]
-    small = small_terms((gq0 + gq1).reshape(heads, hdim), (gk0 + gk1).reshape(heads, hdim), width, shards)
+    part = lambda v: v.reshape(heads, shards, hdim // shards).transpose(1, 0, 2).reshape(shards, -1)
+    small = jnp.concatenate([part(gq0 + gq1), part(gk0 + gk1)], axis=1)
+    small = jnp.pad(small, ((0, 0), (0, low - small.shape[1]))).reshape(width, 1)
     core = (me % 2).astype(jnp.int32).reshape(1)
     keep, send = late_grads(core, gate(left, *n1), [o0, o1], [dq0, dq1], [dk0, dk1], [dv0, dv1], small, low)
-    send = gate(send, *b[2], *b[3], f0[0])
+    send = gate(send, *a, *b[2], *b[3], f0[1])
     f1 = [across(gate(v, send)) for v in n1]
     got = pair(send, 1)
+    keep, send = by_two(keep, got)
+    got = pair(send, 2)
     wb = unpack(mine_b, [(gate(b[0][0], send), b[0][1])] + b[1:])
-    keep, send = by_two(keep, gate(got, wb))
-    got = pair(send, 2)
     gains = gains.reshape(-1, 1)
-    qf, kf, vf, wa, *blank = heads_fwd(mine_a, gate(gains[:inner], send), gains[inner:], left, a, heads, hdim)
+    qf, kf, vf, wa, *blank = heads_fwd(mine_a, gate(gains[:inner], wb), gains[inner:], left, a, heads, hdim)
     of = attend_fwd(qf, kf, vf, vrow, heads, hdim, slots)
     keep = keep + gate(got, of)
     got = to_all(keep)
     outs = out_rows(number[0], gate(x, keep), dz, lng, wout, wa, wb, o0, right, of, n0, f0, cuts, blank)
-    late_rs = cell(keep, 0, me // 4) + sum(gate(v, outs[0]) for v in got)
-    bo, d_in = out_rows(number[1], gate(x, outs[0], *f1), dz, lng, wout, wa, wb, o1, right, of, n1, f1, (0, slots), outs)
-    block_output = bo.reshape(patches.shape)
-    d_in = d_in.reshape(patches.shape)
+    late_rs = cell(keep, 0, me // 4) + sum(got)
     g_w_out = jnp.concatenate([late_rs[:, :inner], early_rs[:, :hidden]], axis=1).T[None]
     g_w_in = jnp.concatenate([late_rs[:, inner : 4 * inner], early_rs[:, hidden:]], axis=1)[None]
     band = lambda v: lax.dynamic_slice_in_dim(v, me * (width // shards), width // shards, 0)
     g_ln = jnp.sum(band(win).astype(F32) * g_w_in[0], axis=1) / band(ln_gain)
+    bo, d_in = out_rows(number[1], gate(x, outs[0], *f1), dz, lng, wout, wa, wb, o1, right, of, n1, f1, (0, slots), outs)
+    block_output = bo.reshape(patches.shape)
+    d_in = d_in.reshape(patches.shape)
     g_ln = g_ln + across(g_ln)
     terms = late_rs[:, 4 * inner]
     count = inner // shards

time: 294 us -> 282 us (0.959); the launches traced: 289 us -> 281 us
  waiting for transfers between devices: 26.2 us -> 20.6 us
  local copies, waits for them, and re-layouts: 22.7 us -> 18.1 us
    ppermute x7 -> x8, waiting for transfers between devices: 10.3 us -> 3.72 us  [per_device(): across = lambda v: lax.ppermute(v, 'head', swap)]
    ppermute x7 -> x8, starting transfers between devices: 9.33 us -> 9.53 us  [per_device(): across = lambda v: lax.ppermute(v, 'head', swap)]
  transfers between devices with their start and end apart: 22 -> 23, of which waited for: 6 -> 7; matrix products, arithmetic and copies ran while one was open for 10% -> 9% of each run, Pallas kernels for 67% -> 69%
where the time goes in v1:
time: 282 us; the launch traced here: 281 us
  Pallas kernels  194 us (69%)
  waiting for transfers between devices  20.6 us (7%)
  starting transfers between devices  19.6 us (7%)
  local copies, waits for them, and re-layouts  18.1 us (6%)
  other arithmetic  14.5 us (5%)
  between operations  14.4 us (5%)
    pallas_call x2, Pallas kernels, attend(): pl.pallas_call(functools.partial(attend_kernel, hdim, min(bq, slots), nh)...  53.4 us
    pallas_call x2, Pallas kernels, out_rows(): pl.pallas_call(functools.partial(out_rows_kernel, inner, cuts, steps), gr...  34.5 us
    pallas_call x1, Pallas kernels, project(): pl.pallas_call(functools.partial(project_kernel, heads, hdim), grid=(step...  24 us
    pallas_call x2, Pallas kernels, back_rows(): pl.pallas_call(functools.partial(back_rows_kernel, inner, cuts, steps), g...  20 us
    ppermute x14, waiting for transfers between devices, pair(): return lax.ppermute(v, 'dp', [(i, i ^ bit) for i in range(shards)])  16.9 us
    pallas_call x1, Pallas kernels, early_grads(): pl.pallas_call(early_kernel, grid=(steps,), in_specs=[pl.BlockSpec((width...  16.3 us
    pallas_call x1, Pallas kernels, late_grads(): pl.pallas_call(functools.partial(late_kernel, seqs, low), grid_spec=pltpu...  14.9 us
    pallas_call x1, Pallas kernels, attend_fwd(): pl.pallas_call(functools.partial(attend_fwd_kernel, hdim, min(bq, slots),...  14.4 us
  transfers between devices with their start and end apart: 23, of which 7 were waited for; matrix products, arithmetic and copies ran while one was open for 9% of the time, Pallas kernels for 69%

profile of v1, /device:TPU:0, one launch (start us, length us, event | category | flops | bytes accessed | tf_op | source)
XLA Modules:
  0.0 281.1 jit_solution(15300740898411426401)
XLA Ops:
  8.0 0.8 reshape.146.qg_ref
  9.0 3.0 %collective-permute-start.1 = (f32[6,128]{1,0:T(8,128)S(1)}, f32[6,128]{1,0:T(8,128)S(1)}, u32[]{:S(2)}, u32[]{:S(2)}) collective-permute-start(f32[6,128]{1,0:T(8,128)S(1)} %bitcast.100), channel_id=1, source_target_pairs={{0,1},{1,0},{2,3},{3,2},{4,5},{5,4},{6,7},{7,6},{8,9},{9,8},{10,11... | collective-permute-start | bytes 9224 | tf_op jit(solution)/shard_map/ppermute | solution.py:565
  12.1 1.1 dynamic-slice_bitcast_fusion
  13.2 1.6 constant_dynamic-slice_fusion.1
  15.3 1.2 slice.54
  17.0 0.8 copy.69.kg_ref
  17.8 1.1 constant_dynamic-slice_fusion
  18.9 1.1 dynamic-slice_bitcast_fusion.1
  20.0 1.0 maximum_convert_fusion.2
  21.7 1.2 maximum_convert_fusion.1
  22.9 24.0 %project.1 = (bf16[1536,2048]{1,0:T(8,128)(2,1)}, bf16[384,2048]{1,0:T(8,128)(2,1)}, bf16[384,2048]{1,0:T(8,128)(2,1)}, bf16[384,2048]{1,0:T(8,128)(2,1)}, bf16[...) custom-call(bf16[2048,768]{1,0:T(8,128)(2,1)} %bitcast.74, ...), custom_call_target="tpu_custom_call" | custom-call | flops 15680000000 | bytes 1 | tf_op jit(solution)/shard_map/project/pallas_call | solution.py:98
  47.6 0.8 collective-permute-done.refs_0_
  49.2 1.5 collective-permute-start.4
  50.7 26.6 %attend.2 = (bf16[1024,384]{1,0:T(8,128)(2,1)}, bf16[1024,384]{1,0:T(8,128)(2,1)}, bf16[1024,384]{1,0:T(8,128)(2,1)}, bf16[1024,384]{1,0:T(8,128)(2,1)}, f32[384,1]{1,0:T(8,128)}, /*index=5*/f32[384,1]{1,0:T(8,128)}) custom-call(s32[1]{0:T(128)} %constant.98.clone.1.image_ref, bf16[384,2048]{1,0:T(8,128)(2,1)} %get-tuple-element.82.qt_ref, ...), custom_call_target="tpu_custom_call" | custom-call | flops 14000000000 | bytes 1 | tf_op jit(solution)/shard_map/attend/pallas_call | solution.py:202
  77.4 1.2 collective-permute-start.3
  78.7 1.5 collective-permute-start.5
  80.1 10.4 %back_rows.2 = (f32[128,768]{1,0:T(8,128)}, f32[896,768]{1,0:T(8,128)}) custom-call(s32[1]{0:T(128)} %constant.98.clone.1.image_ref, bf16[1024,384]{1,0:T(8,128)(2,1)} %get-tuple-element.73.dq_ref.refs_6_, bf16[1024,384]{1,0:T(8,128)(2,1)} %get-tuple-element.74.dk_ref.refs_8_, bf16[1024,384]{1,0:T(8,128)(2,1)} %get-tuple-element.75.dv_ref.refs_10_, ...), custom_call_target="tpu_custom_call" | custom-call | flops 5600000000 | bytes 1 | tf_op jit(solution)/shard_map/back_rows/pallas_call | solution.py:257
  90.5 0.8 collective-permute-start.6
  91.4 16.3 %early_grads.1 = f32[768,3072]{1,0:T(8,128)} custom-call(bf16[1536,2048]{1,0:T(8,128)(2,1)} %get-tuple-element.87.left_ref.refs_0_.refs_1_.refs_2_.refs_3_.xnt_ref, bf16[2048,3072]{1,0:T(8,128)(2,1)} %get-tuple-element.76.du_ref.right_ref.hid_ref), custom_call_target="tpu_custom_call" | custom-call | flops 8960000000 | bytes 1 | tf_op jit(solution)/shard_map/early_grads/pallas_call | solution.py:481
  108.5 0.8 collective-permute-start.14
  109.9 26.8 %attend.3 = (bf16[1024,384]{1,0:T(8,128)(2,1)}, bf16[1024,384]{1,0:T(8,128)(2,1)}, bf16[1024,384]{1,0:T(8,128)(2,1)}, bf16[1024,384]{1,0:T(8,128)(2,1)}, f32[384,1]{1,0:T(8,128)}, /*index=5*/f32[384,1]{1,0:T(8,128)}) custom-call(s32[1]{0:T(128)} %constant.97.clone.1.image_ref, bf16[384,2048]{1,0:T(8,128)(2,1)} %get-tuple-element.82.qt_ref, ...), custom_call_target="tpu_custom_call" | custom-call | flops 14000000000 | bytes 1 | tf_op jit(solution)/shard_map/attend/pallas_call | solution.py:202
  137.8 1.4 add_reduce_fusion
  139.8 1.6 collective-permute-done.11.refs_5_
  141.6 0.9 reshape.147.refs_12_
  142.9 9.7 %back_rows.3.refs_0_ = f32[1024,768]{1,0:T(8,128)} custom-call(s32[1]{0:T(128)} %constant.97.clone.1.image_ref, bf16[1024,384]{1,0:T(8,128)(2,1)} %get-tuple-element.84.dq_ref.refs_7_, bf16[1024,384]{1,0:T(8,128)(2,1)} %get-tuple-element.85.dk_ref.refs_9_, bf16[1024,384]{1,0:T(8,128)(2,1)} %get-tuple-element.86.dv_ref.refs_11_, ...), custom_call_target="tpu_custom_call" | custom-call | flops 5600000000 | bytes 1 | tf_op jit(solution)/shard_map/back_rows/pallas_call | solution.py:257
  152.5 14.9 %late_grads.1 = (f32[384,1664]{1,0:T(8,128)}, f32[384,1664]{1,0:T(8,128)}) custom-call(s32[1]{0:T(128)} %bitcast.1.core_ref, bf16[1536,2048]{1,0:T(8,128)(2,1)} %get-tuple-element.87.left_ref.refs_0_.refs_1_.refs_2_.refs_3_.xnt_ref, bf16[1536,2048]{1,0:T(8,128)(2,1)} %get-tuple-element.87.left_ref.refs_0_.refs_1_.refs_2_.refs_3_.xnt_ref, ...), custom_call_target="tpu_custom_call" | custom-call | flops 6720000000 | bytes 1 | tf_op jit(solution)/shard_map/late_grads/pallas_call | solution.py:529
  168.1 0.8 copy.92
  169.0 0.9 collective-permute-start.17
  169.9 3.3 %collective-permute-done.15 = f32[384,1664]{1,0:T(8,128)S(1)} collective-permute-done((f32[384,1664]{1,0:T(8,128)}, f32[384,1664]{1,0:T(8,128)S(1)}, u32[]{:S(2)}, u32[]{:S(2)}) %collective-permute-start.15) | collective-permute-done | bytes 2555936 | tf_op jit(solution)/shard_map/ppermute | solution.py:568
  173.1 3.5 %add_bitcast_fusion = f32[4,48,1664]{2,1,0:T(8,128)} fusion(f32[4,2,48,1664]{3,2,1,0:T(8,128)S(1)} %bitcast.90, s32[]{:T(128)S(6)} %select_n.75, f32[4,2,48,1664]{3,2,1,0:T(8,128)} %bitcast.88), kind=kLoop, calls=%fused_computation.3 | loop fusion | flops 319488 | bytes 3833860 | tf_op jit(solution)/shard_map/add | solution.py:594
  176.6 1.3 collective-permute-start.16
  178.0 5.8 %unpack.1.wb_ref = bf16[768,3072]{1,0:T(8,128)(2,1)} custom-call(s32[1]{0:T(128)} %bitcast.20.me_ref, f32[112,3072]{1,0:T(8,128)} %collective-permute-done.refs_0_, f32[80,3072]{1,0:T(8,128)} %collective-permute-done.3.refs_1_, f32[112,3072]{1,0:T(8,128)} %collective-permute-done.4.refs_2_, f32[80,3072]{1,0:T(8,128)} %collective-permute-done.7.refs_3_, ...), custom_call_target="tpu_custom_call" | custom-call | flops 3360000000 | bytes 1 | tf_op jit(solution)/shard_map/unpack/pallas_call | solution.py:312
  183.8 0.8 copy.84.qg_ref
  184.6 10.6 %heads_fwd.1 = (bf16[384,2048]{1,0:T(8,128)(2,1)}, bf16[384,2048]{1,0:T(8,128)(2,1)}, bf16[384,2048]{1,0:T(8,128)(2,1)}, bf16[768,384]{1,0:T(8,128)(2,1)}, bf16[...) custom-call(s32[1]{0:T(128)} %bitcast.19.me_ref, f32[384,1]{1,0:T(8,128)} %copy.84.qg_ref, f32[384,1]{1,0:T(8,128)} %bitcast.93, ...), custom_call_target="tpu_custom_call" | custom-call | flops 5600000000 | bytes 1 | tf_op jit(solution)/shard_map/heads_fwd/pallas_call | solution.py:355
  195.3 14.4 %attend_fwd.1.of_ref = bf16[2048,384]{1,0:T(8,128)(2,1)} custom-call(bf16[384,2048]{1,0:T(8,128)(2,1)} %get-tuple-element.105.qt_ref, bf16[384,2048]{1,0:T(8,128)(2,1)} %get-tuple-element.106.kt_ref, bf16[384,2048]{1,0:T(8,128)(2,1)} %get-tuple-element.107.vt_ref, f32[2,1,1024]{2,1,0:T(1,128)} %reshape.144.vrow_ref), custom_call_target="tpu_custom_call" | custom-call | flops 8960000000 | bytes 1 | tf_op jit(solution)/shard_map/attend_fwd/pallas_call | solution.py:400
  209.7 12.0 %collective-permute-done.16 = f32[4,48,1664]{2,1,0:T(8,128)} collective-permute-done((f32[4,48,1664]{2,1,0:T(8,128)}, f32[4,48,1664]{2,1,0:T(8,128)}, u32[]{:S(2)}, u32[]{:S(2)}) %collective-permute-start.16) | collective-permute-done | bytes 1277984 | tf_op jit(solution)/shard_map/ppermute | solution.py:568
  221.7 2.3 fusion.1
  224.1 1.1 copy-done
  225.1 1.0 dynamic-slice_bitcast_fusion.3
  226.1 1.5 collective-permute-start.19
  228.3 1.3 collective-permute-start.18
  229.6 17.2 %out_rows.2 = (bf16[2048,768]{1,0:T(8,128)(2,1)}, bf16[2048,768]{1,0:T(8,128)(2,1)}) custom-call(s32[1]{0:T(128)} %constant.98.clone.1.image_ref, bf16[2048,768]{1,0:T(8,128)(2,1)} %bitcast.76, bf16[2048,768]{1,0:T(8,128)(2,1)} %bitcast.79, f32[1,768]{1,0:T(1,128)} %reshape.124.lng_ref, ...), custom_call_target="tpu_custom_call", output_to_operand_aliasing={{0}: (14, {}), {1}: (15, {})} | custom-call | flops 10080000000 | bytes 1 | tf_op jit(solution)/shard_map/out_rows/pallas_call | solution.py:456
  246.8 17.3 %out_rows.3 = (bf16[2048,768]{1,0:T(8,128)(2,1)}, bf16[2048,768]{1,0:T(8,128)(2,1)}) custom-call(s32[1]{0:T(128)} %constant.97.clone.1.image_ref, bf16[2048,768]{1,0:T(8,128)(2,1)} %bitcast.77, bf16[2048,768]{1,0:T(8,128)(2,1)} %bitcast.80, f32[1,768]{1,0:T(1,128)} %reshape.124.lng_ref, ...), custom_call_target="tpu_custom_call", output_to_operand_aliasing={{0}: (12, {}), {1}: (13, {})} | custom-call | flops 10080000000 | bytes 1 | tf_op jit(solution)/shard_map/out_rows/pallas_call | solution.py:456
  264.1 1.3 bitcast_add_fusion.1
  267.1 1.1 fusion.4
  268.2 1.9 fusion.3
  270.2 1.4 collective-permute-start.21
  272.4 1.3 collective-permute-done.21
  (75 shorter events, 12.2 us)
Async XLA Ops:
  7.2 260.0 %reduce-scatter.2.cloned.1.call-start = ((), (), s32[]{:S(2)}) async-start(), calls=%async_computation.1 | async-start | bytes 10027008 | tf_op jit(solution)/shard_map/reduce_scatter | solution.py:613
  8.8 3.2 %copy-start.2 = (f32[384,1]{1,0:T(8,128)}, f32[384,1]{1,0:T(8,128)S(1)}, u32[]{:S(2)}) copy-start(f32[384,1]{1,0:T(8,128)S(1)} %reshape.146.qg_ref) | copy-start | bytes 4612
  8.9 3.2 %copy-start.3 = (f32[384,1]{1,0:T(8,128)}, f32[384,1]{1,0:T(8,128)S(1)}, u32[]{:S(2)}) copy-start(f32[384,1]{1,0:T(8,128)S(1)} %broadcast_multiply_fusion.qg_ref) | copy-start | bytes 4612
  9.0 40.2 %collective-permute-start.1 = (f32[6,128]{1,0:T(8,128)S(1)}, f32[6,128]{1,0:T(8,128)S(1)}, u32[]{:S(2)}, u32[]{:S(2)}) collective-permute-start(f32[6,128]{1,0:T(8,128)S(1)} %bitcast.100), channel_id=1, source_target_pairs={{0,1},{1,0},{2,3},{3,2},{4,5},{5,4},{6,7},{7,6},{8,9},{9,8},{10,11... | collective-permute-start | bytes 9224 | tf_op jit(solution)/shard_map/ppermute | solution.py:565
  16.5 32.0 %collective-permute-start = (f32[112,3072]{1,0:T(8,128)}, f32[112,3072]{1,0:T(8,128)}, u32[]{:S(2)}, u32[]{:S(2)}) collective-permute-start(f32[112,3072]{1,0:T(8,128)} %slice.54), channel_id=1, source_target_pairs={{0,1},{1,0},{2,3},{3,2},{4,5},{5,4},{6,7},{7,6},{8,9},{9,8},{10,11... | collective-permute-start | bytes 4128776 | tf_op jit(solution)/shard_map/ppermute | solution.py:565
  18.9 2.1 copy-start.5
  22.9 24.0 %copy-start.4 = (s32[2,1024]{1,0:T(2,128)S(1)}, s32[2,1024]{1,0:T(2,128)}, u32[]{:S(2)}) copy-start(s32[2,1024]{1,0:T(2,128)} %param.10) | copy-start | bytes 24580
  22.9 24.0 %copy-start.6 = (s32[2]{0:T(128)S(1)}, s32[2]{0:T(128)}, u32[]{:S(2)}) copy-start(s32[2]{0:T(128)} %param.11) | copy-start | bytes 28
  48.5 28.9 %collective-permute-start.2 = (f32[192,1536]{1,0:T(8,128)}, f32[192,1536]{1,0:T(8,128)}, u32[]{:S(2)}, u32[]{:S(2)}) collective-permute-start(f32[192,1536]{1,0:T(8,128)} %maximum_convert_fusion.1), channel_id=1, source_target_pairs={{0,1},{1,0},{2,3},{3,2},{4,5},{5,4},{6,7},{7,6},{8,9},{9,8},{10,11... | collective-permute-start | bytes 3538952 | tf_op jit(solution)/shard_map/ppermute | solution.py:565
  49.2 58.4 %collective-permute-start.4 = (f32[112,3072]{1,0:T(8,128)}, f32[112,3072]{1,0:T(8,128)}, u32[]{:S(2)}, u32[]{:S(2)}) collective-permute-start(f32[112,3072]{1,0:T(8,128)} %collective-permute-done.refs_0_), channel_id=1, source_target_pairs={{0,8},{2,10},{4,12},{6,14},{8,0},{10,2},{12,4},{14,6},{16,24},{18,... | collective-permute-start | bytes 4128776 | tf_op jit(solution)/shard_map/ppermute | solution.py:568
  77.4 31.1 %collective-permute-start.3 = (f32[80,3072]{1,0:T(8,128)}, f32[80,3072]{1,0:T(8,128)}, u32[]{:S(2)}, u32[]{:S(2)}) collective-permute-start(f32[80,3072]{1,0:T(8,128)} %maximum_convert_fusion.2), channel_id=1, source_target_pairs={{0,1},{1,0},{2,3},{3,2},{4,5},{5,4},{6,7},{7,6},{8,9},{9,8},{10,11... | collective-permute-start | bytes 2949128 | tf_op jit(solution)/shard_map/ppermute | solution.py:565
  78.7 29.8 %collective-permute-start.5 = (f32[192,1536]{1,0:T(8,128)}, f32[192,1536]{1,0:T(8,128)}, u32[]{:S(2)}, u32[]{:S(2)}) collective-permute-start(f32[192,1536]{1,0:T(8,128)} %collective-permute-done.2.refs_0_), channel_id=1, source_target_pairs={{0,4},{2,6},{4,0},{6,2},{8,12},{10,14},{12,8},{14,10},{16,20},{18,... | collective-permute-start | bytes 3538952 | tf_op jit(solution)/shard_map/ppermute | solution.py:568
  90.5 17.9 %collective-permute-start.6 = (f32[128,768]{1,0:T(8,128)}, f32[128,768]{1,0:T(8,128)}, u32[]{:S(2)}, u32[]{:S(2)}) collective-permute-start(f32[128,768]{1,0:T(8,128)} %get-tuple-element.77.refs_0_), channel_id=1, source_target_pairs={{0,1},{1,0},{2,3},{3,2},{4,5},{5,4},{6,7},{7,6},{8,9},{9,8},{10,11... | collective-permute-start | bytes 1179656 | tf_op jit(solution)/shard_map/ppermute | solution.py:565
  108.5 59.6 %collective-permute-start.14 = (f32[896,768]{1,0:T(8,128)}, f32[896,768]{1,0:T(8,128)}, u32[]{:S(2)}, u32[]{:S(2)}) collective-permute-start(f32[896,768]{1,0:T(8,128)} %get-tuple-element.78.refs_1_), channel_id=1, source_target_pairs={{0,1},{1,0},{2,3},{3,2},{4,5},{5,4},{6,7},{7,6},{8,9},{9,8},{10,11... | collective-permute-start | bytes 8257544 | tf_op jit(solution)/shard_map/ppermute | solution.py:565
  109.3 28.0 %collective-permute-start.7 = (f32[80,3072]{1,0:T(8,128)}, f32[80,3072]{1,0:T(8,128)}, u32[]{:S(2)}, u32[]{:S(2)}) collective-permute-start(f32[80,3072]{1,0:T(8,128)} %collective-permute-done.3.refs_1_), channel_id=1, source_target_pairs={{0,8},{2,10},{4,12},{6,14},{8,0},{10,2},{12,4},{14,6},{16,24},{18,... | collective-permute-start | bytes 2949128 | tf_op jit(solution)/shard_map/ppermute | solution.py:568
  136.7 5.8 %collective-permute-start.8 = (f32[192,1536]{1,0:T(8,128)}, f32[192,1536]{1,0:T(8,128)}, u32[]{:S(2)}, u32[]{:S(2)}) collective-permute-start(f32[192,1536]{1,0:T(8,128)} %collective-permute-done.2.refs_0_), channel_id=1, source_target_pairs={{0,2},{2,0},{4,6},{6,4},{8,10},{10,8},{12,14},{14,12},{16,18},{18,... | collective-permute-start | bytes 3538952 | tf_op jit(solution)/shard_map/ppermute | solution.py:568
  136.8 4.6 %collective-permute-start.11 = (f32[80,3072]{1,0:T(8,128)}, f32[80,3072]{1,0:T(8,128)}, u32[]{:S(2)}, u32[]{:S(2)}) collective-permute-start(f32[80,3072]{1,0:T(8,128)} %collective-permute-done.3.refs_1_), channel_id=1, source_target_pairs={{0,2},{2,0},{4,6},{6,4},{8,10},{10,8},{12,14},{14,12},{16,18},{18,... | collective-permute-start | bytes 2949128 | tf_op jit(solution)/shard_map/ppermute | solution.py:568
  137.3 30.1 %collective-permute-start.10 = (f32[112,3072]{1,0:T(8,128)}, f32[112,3072]{1,0:T(8,128)}, u32[]{:S(2)}, u32[]{:S(2)}) collective-permute-start(f32[112,3072]{1,0:T(8,128)} %collective-permute-done.refs_0_), channel_id=1, source_target_pairs={{0,2},{2,0},{4,6},{6,4},{8,10},{10,8},{12,14},{14,12},{16,18},{18,... | collective-permute-start | bytes 4128776 | tf_op jit(solution)/shard_map/ppermute | solution.py:568
  137.3 30.0 %collective-permute-start.12 = (f32[112,3072]{1,0:T(8,128)}, f32[112,3072]{1,0:T(8,128)}, u32[]{:S(2)}, u32[]{:S(2)}) collective-permute-start(f32[112,3072]{1,0:T(8,128)} %collective-permute-done.4.refs_2_), channel_id=1, source_target_pairs={{0,2},{2,0},{4,6},{6,4},{8,10},{10,8},{12,14},{14,12},{16,18},{18,... | collective-permute-start | bytes 4128776 | tf_op jit(solution)/shard_map/ppermute | solution.py:568
  141.3 26.0 %collective-permute-start.9 = (f32[192,1536]{1,0:T(8,128)}, f32[192,1536]{1,0:T(8,128)}, u32[]{:S(2)}, u32[]{:S(2)}) collective-permute-start(f32[192,1536]{1,0:T(8,128)} %collective-permute-done.5.refs_1_), channel_id=1, source_target_pairs={{0,2},{2,0},{4,6},{6,4},{8,10},{10,8},{12,14},{14,12},{16,18},{18,... | collective-permute-start | bytes 3538952 | tf_op jit(solution)/shard_map/ppermute | solution.py:568
  142.5 25.6 %collective-permute-start.13 = (f32[80,3072]{1,0:T(8,128)}, f32[80,3072]{1,0:T(8,128)}, u32[]{:S(2)}, u32[]{:S(2)}) collective-permute-start(f32[80,3072]{1,0:T(8,128)} %collective-permute-done.7.refs_3_), channel_id=1, source_target_pairs={{0,2},{2,0},{4,6},{6,4},{8,10},{10,8},{12,14},{14,12},{16,18},{18,... | collective-permute-start | bytes 2949128 | tf_op jit(solution)/shard_map/ppermute | solution.py:568
  168.1 5.0 %collective-permute-start.15 = (f32[384,1664]{1,0:T(8,128)}, f32[384,1664]{1,0:T(8,128)S(1)}, u32[]{:S(2)}, u32[]{:S(2)}) collective-permute-start(f32[384,1664]{1,0:T(8,128)} %get-tuple-element.102), channel_id=1, source_target_pairs={{0,2},{2,0},{4,6},{6,4},{8,10},{10,8},{12,14},{14,12},{16,18},{18,... | collective-permute-start | bytes 7667720 | tf_op jit(solution)/shard_map/ppermute | solution.py:568
  169.0 77.9 %collective-permute-start.17 = (f32[1024,768]{1,0:T(8,128)}, f32[1024,768]{1,0:T(8,128)}, u32[]{:S(2)}, u32[]{:S(2)}) collective-permute-start(f32[1024,768]{1,0:T(8,128)} %back_rows.3.refs_0_), channel_id=1, source_target_pairs={{0,1},{1,0},{2,3},{3,2},{4,5},{5,4},{6,7},{7,6},{8,9},{9,8},{10,11... | collective-permute-start | bytes 9437192 | tf_op jit(solution)/shard_map/ppermute | solution.py:565
  173.1 3.5 %copy-start.1 = (f32[384,1664]{1,0:T(8,128)}, f32[384,1664]{1,0:T(8,128)S(1)}, u32[]{:S(2)}) copy-start(f32[384,1664]{1,0:T(8,128)S(1)} %collective-permute-done.15) | copy-start | bytes 7667716
  176.6 45.1 %collective-permute-start.16 = (f32[4,48,1664]{2,1,0:T(8,128)}, f32[4,48,1664]{2,1,0:T(8,128)}, u32[]{:S(2)}, u32[]{:S(2)}) collective-permute-start(f32[4,48,1664]{2,1,0:T(8,128)} %add_bitcast_fusion), channel_id=1, source_target_pairs={{0,4},{2,6},{4,0},{6,2},{8,12},{10,14},{12,8},{14,10},{16,20},{18,... | collective-permute-start | bytes 3833864 | tf_op jit(solution)/shard_map/ppermute | solution.py:568
  224.0 1.1 copy-start
  226.1 38.0 %collective-permute-start.19 = (f32[48,1664]{1,0:T(8,128)}, f32[48,1664]{1,0:T(8,128)}, u32[]{:S(2)}, u32[]{:S(2)}) collective-permute-start(f32[48,1664]{1,0:T(8,128)} %get-tuple-element.149), channel_id=1, source_target_pairs={{0,16},{2,18},{4,20},{6,22},{8,24},{10,26},{12,28},{14,30},{16,0},... | collective-permute-start | bytes 958472 | tf_op jit(solution)/shard_map/ppermute | solution.py:568
  227.6 36.5 %collective-permute-start.20 = (f32[48,1664]{1,0:T(8,128)}, f32[48,1664]{1,0:T(8,128)}, u32[]{:S(2)}, u32[]{:S(2)}) collective-permute-start(f32[48,1664]{1,0:T(8,128)} %get-tuple-element.150), channel_id=1, source_target_pairs={{0,24},{2,26},{4,28},{6,30},{8,16},{10,18},{12,20},{14,22},{16,8},... | collective-permute-start | bytes 958472 | tf_op jit(solution)/shard_map/ppermute | solution.py:568
  228.3 35.9 %collective-permute-start.18 = (f32[48,1664]{1,0:T(8,128)}, f32[48,1664]{1,0:T(8,128)}, u32[]{:S(2)}, u32[]{:S(2)}) collective-permute-start(f32[48,1664]{1,0:T(8,128)} %get-tuple-element.151), channel_id=1, source_target_pairs={{0,8},{2,10},{4,12},{6,14},{8,0},{10,2},{12,4},{14,6},{16,24},{18,... | collective-permute-start | bytes 958472 | tf_op jit(solution)/shard_map/ppermute | solution.py:568
  270.2 3.6 %collective-permute-start.21 = (f32[48]{0:T(128)S(1)}, f32[48]{0:T(128)S(1)}, u32[]{:S(2)}, u32[]{:S(2)}) collective-permute-start(f32[48]{0:T(128)S(1)} %dynamic-slice_divide_fusion), channel_id=1, source_target_pairs={{0,1},{1,0},{2,3},{3,2},{4,5},{5,4},{6,7},{7,6},{8,9},{9,8},{10,11... | collective-permute-start | bytes 584 | tf_op jit(solution)/shard_map/ppermute | solution.py:565
Sparse Core Ops, SparseCore 0:
  108.6 139.7 reduce-scatter.1

commit v2 on v1

--- a/solution.py
+++ b/solution.py
@@ -593,8 +593,9 @@
         v, w = (u.reshape(others, 2, low, -1) for u in (v, w))
         return cell(v, 1, bit) + cell(w, 1, bit), cell(v, 1, 1 - bit) + cell(w, 1, 1 - bit)
 
-    def to_all(v):
-        return [pair(cell(v, 0, (me // 4) ^ m), 4 * m) for m in range(1, others)]
+    def to_all(v, w):
+        part = lambda m: cell(v, 0, (me // 4) ^ m) + cell(w, 0, (me // 4) ^ m)
+        return part(0), [pair(part(m), 4 * m) for m in range(1, others)]
 
     def heads_of(s, first):
         return attend(number[s], first, kt, vt, dot, rq, rk, vrow, qg, kg, heads, hdim, slots)
@@ -630,10 +631,9 @@
     gains = gains.reshape(-1, 1)
     qf, kf, vf, wa, *blank = heads_fwd(mine_a, gate(gains[:inner], wb), gains[inner:], left, a, heads, hdim)
     of = attend_fwd(qf, kf, vf, vrow, heads, hdim, slots)
-    keep = keep + gate(got, of)
-    got = to_all(keep)
+    keep, got = to_all(keep, gate(got, of))
     outs = out_rows(number[0], gate(x, keep), dz, lng, wout, wa, wb, o0, right, of, n0, f0, cuts, blank)
-    late_rs = cell(keep, 0, me // 4) + sum(got)
+    late_rs = keep + sum(got)
     g_w_out = jnp.concatenate([late_rs[:, :inner], early_rs[:, :hidden]], axis=1).T[None]
     g_w_in = jnp.concatenate([late_rs[:, inner : 4 * inner], early_rs[:, hidden:]], axis=1)[None]
     band = lambda v: lax.dynamic_slice_in_dim(v, me * (width // shards), width // shards, 0)

time: 282 us -> 310 us (1.099); the launches traced: 281 us -> 305 us
  waiting for transfers between devices: 20.6 us -> 43.9 us
    ppermute x14, waiting for transfers between devices: 16.9 us -> 40 us  [pair(): return lax.ppermute(v, 'dp', [(i, i ^ bit) for i in range(shards)])]
  transfers between devices with their start and end apart: 23 -> 23, of which waited for: 7 -> 8; matrix products, arithmetic and copies ran while one was open for 9% -> 9% of each run, Pallas kernels for 69% -> 64%
where the time goes in v2:
time: 310 us; the launch traced here: 305 us
  Pallas kernels  194 us (63%)
  waiting for transfers between devices  43.9 us (14%)
  starting transfers between devices  19.6 us (6%)
  local copies, waits for them, and re-layouts  16.8 us (5%)
  other arithmetic  16.7 us (5%)
  between operations  14.3 us (5%)
    pallas_call x2, Pallas kernels, attend(): pl.pallas_call(functools.partial(attend_kernel, hdim, min(bq, slots), nh)...  53.3 us
    ppermute x14, waiting for transfers between devices, pair(): return lax.ppermute(v, 'dp', [(i, i ^ bit) for i in range(shards)])  40 us
    pallas_call x2, Pallas kernels, out_rows(): pl.pallas_call(functools.partial(out_rows_kernel, inner, cuts, steps), gr...  34.4 us
    pallas_call x1, Pallas kernels, project(): pl.pallas_call(functools.partial(project_kernel, heads, hdim), grid=(step...  24 us
    pallas_call x2, Pallas kernels, back_rows(): pl.pallas_call(functools.partial(back_rows_kernel, inner, cuts, steps), g...  20 us
    pallas_call x1, Pallas kernels, early_grads(): pl.pallas_call(early_kernel, grid=(steps,), in_specs=[pl.BlockSpec((width...  16.2 us
    pallas_call x1, Pallas kernels, late_grads(): pl.pallas_call(functools.partial(late_kernel, seqs, low), grid_spec=pltpu...  14.9 us
    pallas_call x1, Pallas kernels, attend_fwd(): pl.pallas_call(functools.partial(attend_fwd_kernel, hdim, min(bq, slots),...  14.5 us
  transfers between devices with their start and end apart: 23, of which 8 were waited for; matrix products, arithmetic and copies ran while one was open for 9% of the time, Pallas kernels for 64%

profile of v2, /device:TPU:0, one launch (start us, length us, event | category | flops | bytes accessed | tf_op | source)
XLA Modules:
  0.0 305.0 jit_solution(5630260531308097519)
XLA Ops:
  8.0 0.8 reshape.154.qg_ref
  9.0 3.0 collective-permute-start.1
  12.1 1.1 dynamic-slice_bitcast_fusion
  13.2 1.6 constant_dynamic-slice_fusion.1
  15.3 1.2 slice.54
  17.8 1.1 constant_dynamic-slice_fusion
  18.9 1.1 dynamic-slice_bitcast_fusion.1
  20.0 1.0 maximum_convert_fusion.2
  21.7 1.2 maximum_convert_fusion.1
  22.9 24.0 %project.1 = (bf16[1536,2048]{1,0:T(8,128)(2,1)}, bf16[384,2048]{1,0:T(8,128)(2,1)}, bf16[384,2048]{1,0:T(8,128)(2,1)}, bf16[384,2048]{1,0:T(8,128)(2,1)}, bf16[...) custom-call(bf16[2048,768]{1,0:T(8,128)(2,1)} %bitcast.86, ...), custom_call_target="tpu_custom_call" | custom-call | flops 15680000000 | bytes 1 | tf_op jit(solution)/shard_map/project/pallas_call | solution.py:98
  47.6 0.8 collective-permute-done.refs_0_
  49.2 1.5 collective-permute-start.4
  50.8 26.6 %attend.2 = (bf16[1024,384]{1,0:T(8,128)(2,1)}, bf16[1024,384]{1,0:T(8,128)(2,1)}, bf16[1024,384]{1,0:T(8,128)(2,1)}, bf16[1024,384]{1,0:T(8,128)(2,1)}, f32[384,1]{1,0:T(8,128)}, /*index=5*/f32[384,1]{1,0:T(8,128)}) custom-call(s32[1]{0:T(128)} %constant.118.clone.1.image_ref, bf16[384,2048]{1,0:T(8,128)(2,1)} %get-tuple-element.82.qt_ref, ...), custom_call_target="tpu_custom_call" | custom-call | flops 14000000000 | bytes 1 | tf_op jit(solution)/shard_map/attend/pallas_call | solution.py:202
  77.4 1.2 collective-permute-start.3
  78.6 1.5 collective-permute-start.5
  80.1 10.4 %back_rows.2 = (f32[128,768]{1,0:T(8,128)}, f32[896,768]{1,0:T(8,128)}) custom-call(s32[1]{0:T(128)} %constant.118.clone.1.image_ref, bf16[1024,384]{1,0:T(8,128)(2,1)} %get-tuple-element.73.dq_ref.refs_6_, bf16[1024,384]{1,0:T(8,128)(2,1)} %get-tuple-element.74.dk_ref.refs_8_, bf16[1024,384]{1,0:T(8,128)(2,1)} %get-tuple-element.75.dv_ref.refs_10_, ...), custom_call_target="tpu_custom_call" | custom-call | flops 5600000000 | bytes 1 | tf_op jit(solution)/shard_map/back_rows/pallas_call | solution.py:257
  90.5 0.8 collective-permute-start.6
  91.3 16.2 %early_grads.1 = f32[768,3072]{1,0:T(8,128)} custom-call(bf16[1536,2048]{1,0:T(8,128)(2,1)} %get-tuple-element.87.left_ref.refs_0_.refs_1_.refs_2_.refs_3_.xnt_ref, bf16[2048,3072]{1,0:T(8,128)(2,1)} %get-tuple-element.76.du_ref.right_ref.hid_ref), custom_call_target="tpu_custom_call" | custom-call | flops 8960000000 | bytes 1 | tf_op jit(solution)/shard_map/early_grads/pallas_call | solution.py:481
  107.5 0.9 collective-permute-done.6.refs_2_
  108.5 0.8 collective-permute-start.14
  109.8 26.8 %attend.3 = (bf16[1024,384]{1,0:T(8,128)(2,1)}, bf16[1024,384]{1,0:T(8,128)(2,1)}, bf16[1024,384]{1,0:T(8,128)(2,1)}, bf16[1024,384]{1,0:T(8,128)(2,1)}, f32[384,1]{1,0:T(8,128)}, /*index=5*/f32[384,1]{1,0:T(8,128)}) custom-call(s32[1]{0:T(128)} %constant.117.clone.1.image_ref, bf16[384,2048]{1,0:T(8,128)(2,1)} %get-tuple-element.82.qt_ref, ...), custom_call_target="tpu_custom_call" | custom-call | flops 14000000000 | bytes 1 | tf_op jit(solution)/shard_map/attend/pallas_call | solution.py:202
  137.7 1.4 add_reduce_fusion
  139.7 1.6 collective-permute-done.11.refs_5_
  141.5 0.9 reshape.155.refs_12_
  142.8 9.7 %back_rows.3.refs_0_ = f32[1024,768]{1,0:T(8,128)} custom-call(s32[1]{0:T(128)} %constant.117.clone.1.image_ref, bf16[1024,384]{1,0:T(8,128)(2,1)} %get-tuple-element.84.dq_ref.refs_7_, bf16[1024,384]{1,0:T(8,128)(2,1)} %get-tuple-element.85.dk_ref.refs_9_, bf16[1024,384]{1,0:T(8,128)(2,1)} %get-tuple-element.86.dv_ref.refs_11_, ...), custom_call_target="tpu_custom_call" | custom-call | flops 5600000000 | bytes 1 | tf_op jit(solution)/shard_map/back_rows/pallas_call | solution.py:257
  152.4 14.9 %late_grads.1 = (f32[384,1664]{1,0:T(8,128)}, f32[384,1664]{1,0:T(8,128)}) custom-call(s32[1]{0:T(128)} %bitcast.1.core_ref, bf16[1536,2048]{1,0:T(8,128)(2,1)} %get-tuple-element.87.left_ref.refs_0_.refs_1_.refs_2_.refs_3_.xnt_ref, bf16[1536,2048]{1,0:T(8,128)(2,1)} %get-tuple-element.87.left_ref.refs_0_.refs_1_.refs_2_.refs_3_.xnt_ref, ...), custom_call_target="tpu_custom_call" | custom-call | flops 6720000000 | bytes 1 | tf_op jit(solution)/shard_map/late_grads/pallas_call | solution.py:529
  168.1 0.8 copy.92
  168.9 0.8 collective-permute-start.17
  169.8 3.3 %collective-permute-done.15 = f32[384,1664]{1,0:T(8,128)S(1)} collective-permute-done((f32[384,1664]{1,0:T(8,128)}, f32[384,1664]{1,0:T(8,128)S(1)}, u32[]{:S(2)}, u32[]{:S(2)}) %collective-permute-start.15) | collective-permute-done | bytes 2555936 | tf_op jit(solution)/shard_map/ppermute | solution.py:568
  173.1 3.5 %fusion = f32[4,48,1664]{2,1,0:T(8,128)} fusion(f32[4,2,48,1664]{3,2,1,0:T(8,128)S(1)} %bitcast.102, s32[]{:T(128)S(6)} %select_n.84, f32[4,2,48,1664]{3,2,1,0:T(8,128)} %bitcast.100), kind=kLoop, calls=%fused_computation.1 | loop fusion | flops 319488 | bytes 3833860 | tf_op jit(solution)/shard_map/add | solution.py:594
  176.6 1.3 collective-permute-start.16
  178.0 5.8 %unpack.1.wb_ref = bf16[768,3072]{1,0:T(8,128)(2,1)} custom-call(s32[1]{0:T(128)} %bitcast.20.me_ref, f32[112,3072]{1,0:T(8,128)} %collective-permute-done.refs_0_, f32[80,3072]{1,0:T(8,128)} %collective-permute-done.3.refs_1_, f32[112,3072]{1,0:T(8,128)} %collective-permute-done.4.refs_2_, f32[80,3072]{1,0:T(8,128)} %collective-permute-done.7.refs_3_, ...), custom_call_target="tpu_custom_call" | custom-call | flops 3360000000 | bytes 1 | tf_op jit(solution)/shard_map/unpack/pallas_call | solution.py:312
  183.8 0.8 copy.84.qg_ref
  184.6 10.6 %heads_fwd.1 = (bf16[384,2048]{1,0:T(8,128)(2,1)}, bf16[384,2048]{1,0:T(8,128)(2,1)}, bf16[384,2048]{1,0:T(8,128)(2,1)}, bf16[768,384]{1,0:T(8,128)(2,1)}, bf16[...) custom-call(s32[1]{0:T(128)} %bitcast.19.me_ref, f32[384,1]{1,0:T(8,128)} %copy.84.qg_ref, f32[384,1]{1,0:T(8,128)} %bitcast.105, ...), custom_call_target="tpu_custom_call" | custom-call | flops 5600000000 | bytes 1 | tf_op jit(solution)/shard_map/heads_fwd/pallas_call | solution.py:355
  195.2 2.9 dynamic-slice_add_fusion
  198.1 14.5 %attend_fwd.1.of_ref = bf16[2048,384]{1,0:T(8,128)(2,1)} custom-call(bf16[384,2048]{1,0:T(8,128)(2,1)} %get-tuple-element.105.qt_ref, bf16[384,2048]{1,0:T(8,128)(2,1)} %get-tuple-element.106.kt_ref, bf16[384,2048]{1,0:T(8,128)(2,1)} %get-tuple-element.107.vt_ref, f32[2,1,1024]{2,1,0:T(1,128)} %reshape.152.vrow_ref), custom_call_target="tpu_custom_call" | custom-call | flops 8960000000 | bytes 1 | tf_op jit(solution)/shard_map/attend_fwd/pallas_call | solution.py:400
  212.6 9.2 %collective-permute-done.16 = f32[4,48,1664]{2,1,0:T(8,128)} collective-permute-done((f32[4,48,1664]{2,1,0:T(8,128)}, f32[4,48,1664]{2,1,0:T(8,128)}, u32[]{:S(2)}, u32[]{:S(2)}) %collective-permute-start.16) | collective-permute-done | bytes 1277984 | tf_op jit(solution)/shard_map/ppermute | solution.py:568
  221.8 1.6 fusion.4
  223.4 1.5 collective-permute-start.19
  225.6 1.3 collective-permute-start.18
  226.9 25.9 %collective-permute-done.19 = f32[48,1664]{1,0:T(8,128)S(1)} collective-permute-done((f32[48,1664]{1,0:T(8,128)S(1)}, f32[48,1664]{1,0:T(8,128)S(1)}, u32[]{:S(2)}, u32[]{:S(2)}) %collective-permute-start.19) | collective-permute-done | bytes 319520 | tf_op jit(solution)/shard_map/ppermute | solution.py:568
  252.9 1.2 add_add_fusion
  256.5 17.2 %out_rows.2 = (bf16[2048,768]{1,0:T(8,128)(2,1)}, bf16[2048,768]{1,0:T(8,128)(2,1)}) custom-call(s32[1]{0:T(128)} %constant.118.clone.1.image_ref, bf16[2048,768]{1,0:T(8,128)(2,1)} %bitcast.88, bf16[2048,768]{1,0:T(8,128)(2,1)} %bitcast.91, f32[1,768]{1,0:T(1,128)} %reshape.132.lng_ref, ...), custom_call_target="tpu_custom_call", output_to_operand_aliasing={{0}: (14, {}), {1}: (15, {})} | custom-call | flops 10080000000 | bytes 1 | tf_op jit(solution)/shard_map/out_rows/pallas_call | solution.py:456
  273.7 17.2 %out_rows.3 = (bf16[2048,768]{1,0:T(8,128)(2,1)}, bf16[2048,768]{1,0:T(8,128)(2,1)}) custom-call(s32[1]{0:T(128)} %constant.117.clone.1.image_ref, bf16[2048,768]{1,0:T(8,128)(2,1)} %bitcast.89, bf16[2048,768]{1,0:T(8,128)(2,1)} %bitcast.92, f32[1,768]{1,0:T(1,128)} %reshape.132.lng_ref, ...), custom_call_target="tpu_custom_call", output_to_operand_aliasing={{0}: (12, {}), {1}: (13, {})} | custom-call | flops 10080000000 | bytes 1 | tf_op jit(solution)/shard_map/out_rows/pallas_call | solution.py:456
  291.0 1.1 fusion.8
  292.1 2.0 fusion.2
  294.1 1.5 collective-permute-start.21
  296.4 1.3 collective-permute-done.21
  (76 shorter events, 13.1 us)
Async XLA Ops:
  7.2 283.8 %reduce-scatter.2.cloned.1.call-start = ((), (), s32[]{:S(2)}) async-start(), calls=%async_computation.1 | async-start | bytes 10027008 | tf_op jit(solution)/shard_map/reduce_scatter | solution.py:614
  8.8 3.2 %copy-start.2 = (f32[384,1]{1,0:T(8,128)}, f32[384,1]{1,0:T(8,128)S(1)}, u32[]{:S(2)}) copy-start(f32[384,1]{1,0:T(8,128)S(1)} %reshape.154.qg_ref) | copy-start | bytes 4612
  8.9 3.2 %copy-start.3 = (f32[384,1]{1,0:T(8,128)}, f32[384,1]{1,0:T(8,128)S(1)}, u32[]{:S(2)}) copy-start(f32[384,1]{1,0:T(8,128)S(1)} %broadcast_multiply_fusion.qg_ref) | copy-start | bytes 4612
  9.0 40.2 %collective-permute-start.1 = (f32[6,128]{1,0:T(8,128)S(1)}, f32[6,128]{1,0:T(8,128)S(1)}, u32[]{:S(2)}, u32[]{:S(2)}) collective-permute-start(f32[6,128]{1,0:T(8,128)S(1)} %bitcast.112), channel_id=1, source_target_pairs={{0,1},{1,0},{2,3},{3,2},{4,5},{5,4},{6,7},{7,6},{8,9},{9,8},{10,11... | collective-permute-start | bytes 9224 | tf_op jit(solution)/shard_map/ppermute | solution.py:565
  16.5 32.0 %collective-permute-start = (f32[112,3072]{1,0:T(8,128)}, f32[112,3072]{1,0:T(8,128)}, u32[]{:S(2)}, u32[]{:S(2)}) collective-permute-start(f32[112,3072]{1,0:T(8,128)} %slice.54), channel_id=1, source_target_pairs={{0,1},{1,0},{2,3},{3,2},{4,5},{5,4},{6,7},{7,6},{8,9},{9,8},{10,11... | collective-permute-start | bytes 4128776 | tf_op jit(solution)/shard_map/ppermute | solution.py:565
  18.9 2.1 copy-start.5
  22.9 24.0 %copy-start.4 = (s32[2,1024]{1,0:T(2,128)S(1)}, s32[2,1024]{1,0:T(2,128)}, u32[]{:S(2)}) copy-start(s32[2,1024]{1,0:T(2,128)} %param.10) | copy-start | bytes 24580
  22.9 24.0 %copy-start.6 = (s32[2]{0:T(128)S(1)}, s32[2]{0:T(128)}, u32[]{:S(2)}) copy-start(s32[2]{0:T(128)} %param.11) | copy-start | bytes 28
  48.5 28.9 %collective-permute-start.2 = (f32[192,1536]{1,0:T(8,128)}, f32[192,1536]{1,0:T(8,128)}, u32[]{:S(2)}, u32[]{:S(2)}) collective-permute-start(f32[192,1536]{1,0:T(8,128)} %maximum_convert_fusion.1), channel_id=1, source_target_pairs={{0,1},{1,0},{2,3},{3,2},{4,5},{5,4},{6,7},{7,6},{8,9},{9,8},{10,11... | collective-permute-start | bytes 3538952 | tf_op jit(solution)/shard_map/ppermute | solution.py:565
  49.2 58.3 %collective-permute-start.4 = (f32[112,3072]{1,0:T(8,128)}, f32[112,3072]{1,0:T(8,128)}, u32[]{:S(2)}, u32[]{:S(2)}) collective-permute-start(f32[112,3072]{1,0:T(8,128)} %collective-permute-done.refs_0_), channel_id=1, source_target_pairs={{0,8},{2,10},{4,12},{6,14},{8,0},{10,2},{12,4},{14,6},{16,24},{18,... | collective-permute-start | bytes 4128776 | tf_op jit(solution)/shard_map/ppermute | solution.py:568
  77.4 31.1 %collective-permute-start.3 = (f32[80,3072]{1,0:T(8,128)}, f32[80,3072]{1,0:T(8,128)}, u32[]{:S(2)}, u32[]{:S(2)}) collective-permute-start(f32[80,3072]{1,0:T(8,128)} %maximum_convert_fusion.2), channel_id=1, source_target_pairs={{0,1},{1,0},{2,3},{3,2},{4,5},{5,4},{6,7},{7,6},{8,9},{9,8},{10,11... | collective-permute-start | bytes 2949128 | tf_op jit(solution)/shard_map/ppermute | solution.py:565
  78.6 29.8 %collective-permute-start.5 = (f32[192,1536]{1,0:T(8,128)}, f32[192,1536]{1,0:T(8,128)}, u32[]{:S(2)}, u32[]{:S(2)}) collective-permute-start(f32[192,1536]{1,0:T(8,128)} %collective-permute-done.2.refs_0_), channel_id=1, source_target_pairs={{0,4},{2,6},{4,0},{6,2},{8,12},{10,14},{12,8},{14,10},{16,20},{18,... | collective-permute-start | bytes 3538952 | tf_op jit(solution)/shard_map/ppermute | solution.py:568
  90.5 18.0 %collective-permute-start.6 = (f32[128,768]{1,0:T(8,128)}, f32[128,768]{1,0:T(8,128)}, u32[]{:S(2)}, u32[]{:S(2)}) collective-permute-start(f32[128,768]{1,0:T(8,128)} %get-tuple-element.77.refs_0_), channel_id=1, source_target_pairs={{0,1},{1,0},{2,3},{3,2},{4,5},{5,4},{6,7},{7,6},{8,9},{9,8},{10,11... | collective-permute-start | bytes 1179656 | tf_op jit(solution)/shard_map/ppermute | solution.py:565
  108.5 59.6 %collective-permute-start.14 = (f32[896,768]{1,0:T(8,128)}, f32[896,768]{1,0:T(8,128)}, u32[]{:S(2)}, u32[]{:S(2)}) collective-permute-start(f32[896,768]{1,0:T(8,128)} %get-tuple-element.78.refs_1_), channel_id=1, source_target_pairs={{0,1},{1,0},{2,3},{3,2},{4,5},{5,4},{6,7},{7,6},{8,9},{9,8},{10,11... | collective-permute-start | bytes 8257544 | tf_op jit(solution)/shard_map/ppermute | solution.py:565
  109.3 28.0 %collective-permute-start.7 = (f32[80,3072]{1,0:T(8,128)}, f32[80,3072]{1,0:T(8,128)}, u32[]{:S(2)}, u32[]{:S(2)}) collective-permute-start(f32[80,3072]{1,0:T(8,128)} %collective-permute-done.3.refs_1_), channel_id=1, source_target_pairs={{0,8},{2,10},{4,12},{6,14},{8,0},{10,2},{12,4},{14,6},{16,24},{18,... | collective-permute-start | bytes 2949128 | tf_op jit(solution)/shard_map/ppermute | solution.py:568
  136.6 5.8 %collective-permute-start.8 = (f32[192,1536]{1,0:T(8,128)}, f32[192,1536]{1,0:T(8,128)}, u32[]{:S(2)}, u32[]{:S(2)}) collective-permute-start(f32[192,1536]{1,0:T(8,128)} %collective-permute-done.2.refs_0_), channel_id=1, source_target_pairs={{0,2},{2,0},{4,6},{6,4},{8,10},{10,8},{12,14},{14,12},{16,18},{18,... | collective-permute-start | bytes 3538952 | tf_op jit(solution)/shard_map/ppermute | solution.py:568
  136.7 4.6 %collective-permute-start.11 = (f32[80,3072]{1,0:T(8,128)}, f32[80,3072]{1,0:T(8,128)}, u32[]{:S(2)}, u32[]{:S(2)}) collective-permute-start(f32[80,3072]{1,0:T(8,128)} %collective-permute-done.3.refs_1_), channel_id=1, source_target_pairs={{0,2},{2,0},{4,6},{6,4},{8,10},{10,8},{12,14},{14,12},{16,18},{18,... | collective-permute-start | bytes 2949128 | tf_op jit(solution)/shard_map/ppermute | solution.py:568
  137.2 30.1 %collective-permute-start.10 = (f32[112,3072]{1,0:T(8,128)}, f32[112,3072]{1,0:T(8,128)}, u32[]{:S(2)}, u32[]{:S(2)}) collective-permute-start(f32[112,3072]{1,0:T(8,128)} %collective-permute-done.refs_0_), channel_id=1, source_target_pairs={{0,2},{2,0},{4,6},{6,4},{8,10},{10,8},{12,14},{14,12},{16,18},{18,... | collective-permute-start | bytes 4128776 | tf_op jit(solution)/shard_map/ppermute | solution.py:568
  137.3 30.1 %collective-permute-start.12 = (f32[112,3072]{1,0:T(8,128)}, f32[112,3072]{1,0:T(8,128)}, u32[]{:S(2)}, u32[]{:S(2)}) collective-permute-start(f32[112,3072]{1,0:T(8,128)} %collective-permute-done.4.refs_2_), channel_id=1, source_target_pairs={{0,2},{2,0},{4,6},{6,4},{8,10},{10,8},{12,14},{14,12},{16,18},{18,... | collective-permute-start | bytes 4128776 | tf_op jit(solution)/shard_map/ppermute | solution.py:568
  141.3 26.0 %collective-permute-start.9 = (f32[192,1536]{1,0:T(8,128)}, f32[192,1536]{1,0:T(8,128)}, u32[]{:S(2)}, u32[]{:S(2)}) collective-permute-start(f32[192,1536]{1,0:T(8,128)} %collective-permute-done.5.refs_1_), channel_id=1, source_target_pairs={{0,2},{2,0},{4,6},{6,4},{8,10},{10,8},{12,14},{14,12},{16,18},{18,... | collective-permute-start | bytes 3538952 | tf_op jit(solution)/shard_map/ppermute | solution.py:568
  142.4 25.7 %collective-permute-start.13 = (f32[80,3072]{1,0:T(8,128)}, f32[80,3072]{1,0:T(8,128)}, u32[]{:S(2)}, u32[]{:S(2)}) collective-permute-start(f32[80,3072]{1,0:T(8,128)} %collective-permute-done.7.refs_3_), channel_id=1, source_target_pairs={{0,2},{2,0},{4,6},{6,4},{8,10},{10,8},{12,14},{14,12},{16,18},{18,... | collective-permute-start | bytes 2949128 | tf_op jit(solution)/shard_map/ppermute | solution.py:568
  168.1 5.0 %collective-permute-start.15 = (f32[384,1664]{1,0:T(8,128)}, f32[384,1664]{1,0:T(8,128)S(1)}, u32[]{:S(2)}, u32[]{:S(2)}) collective-permute-start(f32[384,1664]{1,0:T(8,128)} %get-tuple-element.102), channel_id=1, source_target_pairs={{0,2},{2,0},{4,6},{6,4},{8,10},{10,8},{12,14},{14,12},{16,18},{18,... | collective-permute-start | bytes 7667720 | tf_op jit(solution)/shard_map/ppermute | solution.py:568
  168.9 104.7 %collective-permute-start.17 = (f32[1024,768]{1,0:T(8,128)}, f32[1024,768]{1,0:T(8,128)}, u32[]{:S(2)}, u32[]{:S(2)}) collective-permute-start(f32[1024,768]{1,0:T(8,128)} %back_rows.3.refs_0_), channel_id=1, source_target_pairs={{0,1},{1,0},{2,3},{3,2},{4,5},{5,4},{6,7},{7,6},{8,9},{9,8},{10,11... | collective-permute-start | bytes 9437192 | tf_op jit(solution)/shard_map/ppermute | solution.py:565
  173.1 3.5 %copy-start = (f32[384,1664]{1,0:T(8,128)}, f32[384,1664]{1,0:T(8,128)S(1)}, u32[]{:S(2)}) copy-start(f32[384,1664]{1,0:T(8,128)S(1)} %collective-permute-done.15) | copy-start | bytes 7667716
  176.6 45.1 %collective-permute-start.16 = (f32[4,48,1664]{2,1,0:T(8,128)}, f32[4,48,1664]{2,1,0:T(8,128)}, u32[]{:S(2)}, u32[]{:S(2)}) collective-permute-start(f32[4,48,1664]{2,1,0:T(8,128)} %fusion), channel_id=1, source_target_pairs={{0,4},{2,6},{4,0},{6,2},{8,12},{10,14},{12,8},{14,10},{16,20},{18,... | collective-permute-start | bytes 3833864 | tf_op jit(solution)/shard_map/ppermute | solution.py:568
  223.4 29.5 %collective-permute-start.19 = (f32[48,1664]{1,0:T(8,128)S(1)}, f32[48,1664]{1,0:T(8,128)S(1)}, u32[]{:S(2)}, u32[]{:S(2)}) collective-permute-start(f32[48,1664]{1,0:T(8,128)S(1)} %get-tuple-element.151), channel_id=1, source_target_pairs={{0,16},{2,18},{4,20},{6,22},{8,24},{10,26},{12,28},{14,30},{16,0},... | collective-permute-start | bytes 958472 | tf_op jit(solution)/shard_map/ppermute | solution.py:568
  224.9 28.0 %collective-permute-start.20 = (f32[48,1664]{1,0:T(8,128)S(1)}, f32[48,1664]{1,0:T(8,128)S(1)}, u32[]{:S(2)}, u32[]{:S(2)}) collective-permute-start(f32[48,1664]{1,0:T(8,128)S(1)} %get-tuple-element.152), channel_id=1, source_target_pairs={{0,24},{2,26},{4,28},{6,30},{8,16},{10,18},{12,20},{14,22},{16,8},... | collective-permute-start | bytes 958472 | tf_op jit(solution)/shard_map/ppermute | solution.py:568
  225.6 27.3 %collective-permute-start.18 = (f32[48,1664]{1,0:T(8,128)S(1)}, f32[48,1664]{1,0:T(8,128)S(1)}, u32[]{:S(2)}, u32[]{:S(2)}) collective-permute-start(f32[48,1664]{1,0:T(8,128)S(1)} %get-tuple-element.153), channel_id=1, source_target_pairs={{0,8},{2,10},{4,12},{6,14},{8,0},{10,2},{12,4},{14,6},{16,24},{18,... | collective-permute-start | bytes 958472 | tf_op jit(solution)/shard_map/ppermute | solution.py:568
  254.1 0.8 copy-start.1
  290.9 4.7 %slice-start = ((f32[48,1664]{1,0:T(8,128)}), f32[48,384]{1,0:T(8,128)S(1)}, s32[]{:S(2)}) async-start(f32[48,1664]{1,0:T(8,128)} %copy-done.1), calls=%async_computation.2 | async-start | bytes 147456 | tf_op jit(solution)/shard_map/slice | solution.py:637
  294.1 3.6 %collective-permute-start.21 = (f32[48]{0:T(128)S(1)}, f32[48]{0:T(128)S(1)}, u32[]{:S(2)}, u32[]{:S(2)}) collective-permute-start(f32[48]{0:T(128)S(1)} %dynamic-slice_divide_fusion), channel_id=1, source_target_pairs={{0,1},{1,0},{2,3},{3,2},{4,5},{5,4},{6,7},{7,6},{8,9},{9,8},{10,11... | collective-permute-start | bytes 584 | tf_op jit(solution)/shard_map/ppermute | solution.py:565
Sparse Core Ops, SparseCore 0:
  108.6 141.4 reduce-scatter.1
